TPU v7x, 128 devices: a whole 4x4x4 slice. The times are simulated.
128 devices in a mesh: expert: 8 (over z_lo, x), shard: 16 (over z_hi, y, core).
Axes of the slice: x: 4, y: 4, z: 4 (z_hi: 2, z_lo: 2; z = z_hi * 2 + z_lo), core: 2. Of those that a mesh axis runs over, the one named last changes fastest.
Arguments:
- grad_out: bfloat16 [8, 2048, 3072], P('expert', 'shard'), may hold values from -6 to 6
- gate_pre: bfloat16 [8, 2048, 8192], P('expert', None, 'shard'), may hold values from -8 to 8
- up_pre: bfloat16 [8, 2048, 8192], P('expert', None, 'shard'), may hold values from -6 to 6
- counts: int32 [8, 16], P('expert', 'shard'), may hold values from 32 to 128
- placement: int32 [8], replicated, may hold values from 0 to 63, as said below
- master: float32 [8, 8192, 3072], P('expert', 'shard')
Outputs:
- d_gate: bfloat16 [8, 2048, 8192], P('expert', None, 'shard')
- d_up: bfloat16 [8, 2048, 8192], P('expert', None, 'shard')
- new_master: float32 [8, 8192, 3072], P('expert', 'shard')
Inputs may be any that keep to these rules, and one draw needn't show every extreme that they name: `placement`: slots that hold the same expert form aligned blocks of 1, 2 or 4 consecutive slots, each block starting at a multiple of its size; different blocks hold different experts.
All inputs are finite; a program needn't handle non-finite values.
Results may differ from a plain program's by a relative error of at most 0.006.
Values may be sent and summed in bfloat16 or wider, within the bound.
A program may use at most 256 MiB of HBM per device.

v0:
```python
import jax
import jax.numpy as jnp
from jax import lax
from jax.sharding import PartitionSpec as P

learn_rate = 0.02
rms_eps = 1e-06


def from_partner(shard, axis, bit):
    return lax.ppermute(shard, axis, [(i, i ^ 1 << bit) for i in range(lax.axis_size(axis))])


def per_device(grad_out, gate_pre, up_pre, counts, placement, master):
    weight_work = master[0].astype(jnp.bfloat16)
    local_rows = grad_out.shape[1]
    row_valid = (jnp.arange(local_rows, dtype=jnp.int32) < counts[0, 0]).astype(jnp.bfloat16)
    masked = grad_out[0] * row_valid[:, None]
    gate_val = gate_pre[0].astype(jnp.float32)
    up_val = up_pre[0].astype(jnp.float32)
    gate_sig = jax.nn.sigmoid(gate_val)
    gate_act = gate_val * gate_sig
    gate_slope = gate_sig * (1.0 + gate_val * (1.0 - gate_sig))
    hidden = (gate_act * up_val).astype(jnp.bfloat16)
    my_slot = lax.axis_index("expert")
    slot_order = jnp.arange(placement.shape[0], dtype=jnp.int32)
    my_expert = jnp.sum(jnp.where(slot_order == my_slot, placement, 0))
    block_rows = lax.all_gather(masked, "shard", axis=0, tiled=True)
    d_hidden = lax.dot_general(
        block_rows, weight_work, (((1,), (1,)), ((), ())), preferred_element_type=jnp.float32
    )
    up_acc = (d_hidden * gate_act).astype(jnp.bfloat16)
    gate_acc = (d_hidden * up_val * gate_slope).astype(jnp.bfloat16)
    grad_acc = lax.dot_general(
        hidden, block_rows, (((0,), (0,)), ((), ())), preferred_element_type=jnp.float32
    )
    grad_sum = grad_acc
    for bit_pos in range(2):
        received = from_partner(grad_sum.astype(jnp.bfloat16), "expert", bit_pos).astype(
            grad_sum.dtype
        )
        other_slot = jnp.bitwise_xor(my_slot, 1 << bit_pos)
        their_expert = jnp.sum(jnp.where(slot_order == other_slot, placement, 0))
        grad_sum = grad_sum + jnp.where(my_expert == their_expert, received, 0.0)
    row_rms = jnp.sqrt(jnp.mean(grad_sum * grad_sum, axis=1, keepdims=True) + rms_eps)
    new_master = master[0] - learn_rate * grad_sum / row_rms
    return (gate_acc[None], up_acc[None], new_master[None])


def solution(mesh):
    return jax.shard_map(
        per_device,
        mesh=mesh,
        in_specs=(
            P("expert", "shard", None),
            P("expert", None, "shard"),
            P("expert", None, "shard"),
            P("expert", "shard"),
            P(),
            P("expert", "shard", None),
        ),
        out_specs=(
            P("expert", None, "shard"),
            P("expert", None, "shard"),
            P("expert", "shard", None),
        ),
        check_vma=False,
    )
```

profile of v0, /device:TPU:0, one launch (start us, length us, event | category | flops | bytes accessed | tf_op | source)
XLA Modules:
  0.0 284.9 jit_solution(8563610116932885319)
XLA Ops:
  7.2 0.0 all-gather.2.cloned.1.call-start
  7.9 2.1 bitcast_multiply_fusion
  10.0 0.0 all-gather.2.cloned.1.call-update
  10.0 0.0 copy-start.2
  10.0 94.5 %all-gather.2.cloned.1.call-done = bf16[2048,3072]{1,0:T(8,128)(2,1)} async-done(((bf16[128,3072]{1,0:T(8,128)(2,1)}), bf16[2048,3072]{1,0:T(8,128)(2,1)}) %all-gather.2.cloned.1.call-update) | async-done | bytes 12582928 | tf_op jit(solution)/shard_map/all_gather | solution.py:28
  104.5 13.4 %fusion.21 = (bf16[512,3072]{1,0:T(8,128)(2,1)}, f32[512,3072]{1,0:T(8,128)}) fusion(bf16[2048,3072]{1,0:T(8,128)(2,1)} %all-gather.2.cloned.1.call-done, bf16[1,2048,512]{2,1,0:T(8,128)(2,1)} %param.8, bf16[1,2048,512]{2,1,0:T(8,128)(2,1)} %param.7), kind=kOutput, calls=%fused_computation.36 | convolution fusion | flops 6452412416 | bytes 26214400 | tf_op jit(solution)/shard_map/dot_general | solution.py:34
  117.9 1.5 collective-permute-start
  119.4 0.0 copy-done.2
  119.4 0.7 fusion.18
  121.5 66.9 %collective-permute-done = bf16[512,3072]{1,0:T(8,128)(2,1)S(1)} collective-permute-done((bf16[512,3072]{1,0:T(8,128)(2,1)}, bf16[512,3072]{1,0:T(8,128)(2,1)S(1)}, u32[]{:S(2)}, u32[]{:S(2)}) %collective-permute-start) | collective-permute-done | bytes 3145760 | tf_op jit(solution)/shard_map/ppermute | solution.py:11
  188.4 0.0 copy-start
  188.4 1.6 copy-done
  190.1 0.0 slice-start
  190.1 6.6 %fusion.9 = bf16[512,3072]{1,0:T(8,128)(2,1)} fusion(f32[512,3072]{1,0:T(8,128)} %get-tuple-element.9, bf16[512,3072]{1,0:T(8,128)(2,1)} %copy-done, pred[]{:T(512)S(6)} %eq.28), kind=kLoop, calls=%fused_computation.20 | loop fusion | flops 6291456 | bytes 12582913 | tf_op jit(solution)/shard_map/convert_element_type | solution.py:39
  196.6 3.0 %collective-permute-start.1 = (bf16[512,3072]{1,0:T(8,128)(2,1)}, bf16[512,3072]{1,0:T(8,128)(2,1)}, u32[]{:S(2)}, u32[]{:S(2)}) collective-permute-start(bf16[512,3072]{1,0:T(8,128)(2,1)} %fusion.9), channel_id=1, source_target_pairs={{0,32},{16,48},{32,0},{48,16},{64,96},{80,112},{96,64},{112,80},{1... | collective-permute-start | bytes 9437192 | tf_op jit(solution)/shard_map/ppermute | solution.py:11
  200.9 0.0 slice-start.1
  200.9 0.0 copy-start.1
  200.9 16.6 %fusion.11 = (bf16[1,2048,512]{2,1,0:T(8,128)(2,1)}, bf16[1,2048,512]{2,1,0:T(8,128)(2,1)}) fusion(bf16[1,2048,512]{2,1,0:T(8,128)(2,1)} %param.7, bf16[1,2048,512]{2,1,0:T(8,128)(2,1)} %param.8, bf16[2048,3072]{1,0:T(8,128)(2,1)} %all-gather.2.cloned.1.call-done, f32[1,512,3072]{2,1,0:T(8,128)} %param.11), kind=kOutput, calls=%fused_computation.22 | convolution fusion | flops 6458179584 | bytes 27262976 | tf_op jit(solution)/shard_map/dot_general | solution.py:29
  217.5 50.4 %collective-permute-done.1 = bf16[512,3072]{1,0:T(8,128)(2,1)} collective-permute-done((bf16[512,3072]{1,0:T(8,128)(2,1)}, bf16[512,3072]{1,0:T(8,128)(2,1)}, u32[]{:S(2)}, u32[]{:S(2)}) %collective-permute-start.1) | collective-permute-done | bytes 3145760 | tf_op jit(solution)/shard_map/ppermute | solution.py:11
  267.9 0.0 slice-done
  267.9 0.0 slice-done.1
  267.9 0.0 copy-done.1
  267.9 3.6 %multiply_reduce_fusion = f32[512]{0:T(512)S(1)} fusion(bf16[512,3072]{1,0:T(8,128)(2,1)} %collective-permute-done.1, pred[]{:T(512)S(6)} %eq.31, f32[512,3072]{1,0:T(8,128)S(1)} %bitcast.54, bf16[512,3072]{1,0:T(8,128)(2,1)S(1)} %copy-done.1, pred[]{:T(512)S(6)} %eq.28), kind=kLoop, calls=%fused_computation.6 | loop fusion | flops 12582400 | bytes 12584962 | tf_op jit(solution)/shard_map/reduce_sum | solution.py:45
  271.6 6.5 %fusion = f32[1,512,3072]{2,1,0:T(8,128)} fusion(f32[1,512,3072]{2,1,0:T(8,128)} %param.11, f32[512]{0:T(512)S(1)} %add_sqrt_fusion, bf16[512,3072]{1,0:T(8,128)(2,1)} %collective-permute-done.1, pred[]{:T(512)S(6)} %eq.31, f32[512,3072]{1,0:T(8,128)S(1)} %bitcast.54, bf16[512,3072]{1,0:T(8,128)(2,1)S(1)} %copy-done.1, pred[]{:T(512)S(6)} %eq.28), kind=kLoop, calls=%fused_computation.5 | loop fusion | flops 14155776 | bytes 25167874 | tf_op jit(solution)/shard_map/broadcast_in_dim | solution.py:47
  (3 shorter events, 0.0 us)
Async XLA Ops:
  7.2 97.4 %all-gather.2.cloned.1.call-start = ((), (), s32[]{:S(2)}) async-start(), calls=%async_computation | async-start | bytes 13369344 | tf_op jit(solution)/shard_map/all_gather | solution.py:28
  10.0 109.4 %copy-start.2 = (s32[8]{0:T(128)S(1)}, s32[8]{0:T(128)}, u32[]{:S(2)}) copy-start(s32[8]{0:T(128)} %param.10) | copy-start | bytes 100
  117.9 70.5 %collective-permute-start = (bf16[512,3072]{1,0:T(8,128)(2,1)}, bf16[512,3072]{1,0:T(8,128)(2,1)S(1)}, u32[]{:S(2)}, u32[]{:S(2)}) collective-permute-start(bf16[512,3072]{1,0:T(8,128)(2,1)} %get-tuple-element.8), channel_id=1, source_target_pairs={{0,16},{16,0},{32,48},{48,32},{64,80},{80,64},{96,112},{112,96},{1... | collective-permute-start | bytes 9437192 | tf_op jit(solution)/shard_map/ppermute | solution.py:11
  188.4 1.6 copy-start
  190.1 77.8 %slice-start = ((s8[6291456]{0:T(1024)(128)(4,1)}), s8[2097152]{0:T(1024)(128)(4,1)S(1)}, s32[]{:S(2)}) async-start(s8[6291456]{0:T(1024)(128)(4,1)} %bitcast.53), calls=%async_computation.1 | async-start | bytes 4194304
  196.6 71.3 %collective-permute-start.1 = (bf16[512,3072]{1,0:T(8,128)(2,1)}, bf16[512,3072]{1,0:T(8,128)(2,1)}, u32[]{:S(2)}, u32[]{:S(2)}) collective-permute-start(bf16[512,3072]{1,0:T(8,128)(2,1)} %fusion.9), channel_id=1, source_target_pairs={{0,32},{16,48},{32,0},{48,16},{64,96},{80,112},{96,64},{112,80},{1... | collective-permute-start | bytes 9437192 | tf_op jit(solution)/shard_map/ppermute | solution.py:11
  200.9 67.0 %slice-start.1 = ((s8[6291456]{0:T(1024)(128)(4,1)}), s8[4194304]{0:T(1024)(128)(4,1)S(1)}, s32[]{:S(2)}) async-start(s8[6291456]{0:T(1024)(128)(4,1)} %bitcast.53), calls=%async_computation.2 | async-start | bytes 8388608
  200.9 67.0 %copy-start.1 = (bf16[512,3072]{1,0:T(8,128)(2,1)S(1)}, bf16[512,3072]{1,0:T(8,128)(2,1)}, u32[]{:S(2)}) copy-start(bf16[512,3072]{1,0:T(8,128)(2,1)} %copy-done) | copy-start | bytes 9437188
Sparse Core Ops, SparseCore 0:
  11.0 93.4 all-gather.1
where the time goes:
time: 285 us
  waiting for transfers between devices  212 us (74%)
  matrix products  30 us (11%)
  other arithmetic  19.6 us (7%)
  between operations  17.4 us (6%)
  starting transfers between devices  4.49 us (2%)
    ppermute x2, waiting for transfers between devices, from_partner(): lax.ppermute(shard, axis, [(i, i ^ 1 << bit) for i in range(lax.axis_size...  117 us
    all_gather x1, waiting for transfers between devices, per_device(): block_rows = lax.all_gather(masked, 'shard', axis=0, tiled=True)  94.5 us
    dot_general x1, matrix products, per_device(): lax.dot_general(block_rows, weight_work, (((1,), (1,)), ((), ())), prefer...  16.6 us
    dot_general x1, matrix products, per_device(): lax.dot_general(hidden, block_rows, (((0,), (0,)), ((), ())), preferred_e...  13.4 us
    convert_element_type x1, other arithmetic, per_device(): grad_sum.astype(jnp.bfloat16)  6.56 us
    broadcast_in_dim x1, other arithmetic, per_device(): return (gate_acc[None], up_acc[None], new_master[None])  6.48 us
  transfers between devices with their start and end apart: 3, of which 3 were waited for; matrix products, arithmetic and copies ran while one was open for 6% of the time, Pallas kernels for 0%

commit v1 on v0

v1 whole, which is shorter than its diff:
```python
import jax
import jax.numpy as jnp
from jax import lax
from jax.sharding import PartitionSpec as P

learn_rate = 0.02
rms_eps = 1e-06
pieces = 6


def from_partner(shard, axis, flip):
    return lax.ppermute(shard, axis, [(i, i ^ flip) for i in range(lax.axis_size(axis))])


def per_device(grad_out, gate_pre, up_pre, counts, placement, master):
    weight_work = master[0].astype(jnp.bfloat16)
    local_rows, width = grad_out.shape[1], grad_out.shape[2]
    row_valid = (jnp.arange(local_rows, dtype=jnp.int32) < counts[0, 0]).astype(jnp.bfloat16)
    masked = grad_out[0] * row_valid[:, None]
    gate_val = gate_pre[0].astype(jnp.float32)
    up_val = up_pre[0].astype(jnp.float32)
    gate_sig = jax.nn.sigmoid(gate_val)
    gate_act = gate_val * gate_sig
    gate_slope = gate_sig * (1.0 + gate_val * (1.0 - gate_sig))
    hidden = (gate_act * up_val).astype(jnp.bfloat16)
    my_slot = lax.axis_index("expert")
    slot_order = jnp.arange(placement.shape[0], dtype=jnp.int32)

    def expert_of(slot):
        return jnp.sum(jnp.where(slot_order == slot, placement, 0))

    my_expert = expert_of(my_slot)
    same_pair = my_expert == expert_of(my_slot ^ 1)
    same_quad = my_expert == expert_of(my_slot ^ 3)
    step = width // pieces
    d_hidden = 0.0
    sums = []
    for piece in range(pieces):
        cols = slice(piece * step, (piece + 1) * step)
        rows = lax.all_gather(masked[:, cols], "shard", axis=0, tiled=True)
        grad = lax.dot_general(
            hidden, rows, (((0,), (0,)), ((), ())), preferred_element_type=jnp.float32
        )
        for flip, same in ((1, same_pair), (3, same_quad)):
            received = from_partner(grad.astype(jnp.bfloat16), "expert", flip)
            grad = grad + jnp.where(same, received.astype(jnp.float32), 0.0)
        sums.append(grad)
        d_hidden = d_hidden + lax.dot_general(
            rows, weight_work[:, cols], (((1,), (1,)), ((), ())), preferred_element_type=jnp.float32
        )
    up_acc = (d_hidden * gate_act).astype(jnp.bfloat16)
    gate_acc = (d_hidden * up_val * gate_slope).astype(jnp.bfloat16)
    grad_sum = jnp.concatenate(sums, axis=1)
    row_rms = jnp.sqrt(jnp.mean(grad_sum * grad_sum, axis=1, keepdims=True) + rms_eps)
    new_master = master[0] - learn_rate * grad_sum / row_rms
    return (gate_acc[None], up_acc[None], new_master[None])


def solution(mesh):
    return jax.shard_map(
        per_device,
        mesh=mesh,
        in_specs=(
            P("expert", "shard", None),
            P("expert", None, "shard"),
            P("expert", None, "shard"),
            P("expert", "shard"),
            P(),
            P("expert", "shard", None),
        ),
        out_specs=(
            P("expert", None, "shard"),
            P("expert", None, "shard"),
            P("expert", "shard", None),
        ),
        check_vma=False,
    )
```

time: 285 us -> 442 us (1.55)
  waiting for transfers between devices: 212 us -> 327 us
  starting transfers between devices: 4.49 us -> 22.1 us
  local copies, waits for them, and re-layouts: 1.67 us -> 15.8 us
  matrix products: 30 us -> 44.1 us
  other arithmetic: 19.6 us -> 14.4 us
    all_gather x1 -> x6, waiting for transfers between devices: 94.5 us -> 259 us  [per_device(): rows = lax.all_gather(masked[:, cols], 'shard', axis=0, tiled=True)]
    ppermute x2 -> x12, waiting for transfers between devices: 117 us -> 65.3 us  [from_partner(): lax.ppermute(shard, axis, [(i, i ^ flip) for i in range(lax.axis_size(axi...]
    ppermute x2 -> x12, starting transfers between devices: 4.45 us -> 21.9 us  [from_partner(): lax.ppermute(shard, axis, [(i, i ^ flip) for i in range(lax.axis_size(axi...]
    dot_general x2 -> x12, matrix products: 30 us -> 44.1 us  [the longest x6 36.3 us: per_device(): lax.dot_general(rows, weight_work[:, cols], (((1,), (1,)), ((), ())), pre...]
    unnamed x10 -> x18, local copies, waits for them, and re-layouts: 1.67 us -> 14.9 us
    broadcast_in_dim x1 -> x0, other arithmetic: 6.48 us -> none  [per_device(): return (gate_acc[None], up_acc[None], new_master[None])]
  transfers between devices with their start and end apart: 3 -> 18, of which waited for: 3 -> 14; matrix products, arithmetic and copies ran while one was open for 6% -> 10% of each run, Pallas kernels for 0% -> 0%
where the time goes in v1:
time: 442 us; the launch traced here: 441 us
  waiting for transfers between devices  327 us (74%)
  matrix products  44.1 us (10%)
  starting transfers between devices  22.1 us (5%)
  between operations  17.6 us (4%)
  local copies, waits for them, and re-layouts  15.8 us (4%)
  other arithmetic  14.4 us (3%)
    all_gather x6, waiting for transfers between devices, per_device(): rows = lax.all_gather(masked[:, cols], 'shard', axis=0, tiled=True)  259 us
    ppermute x12, waiting for transfers between devices, from_partner(): lax.ppermute(shard, axis, [(i, i ^ flip) for i in range(lax.axis_size(axi...  65.3 us
    dot_general x6, matrix products, per_device(): lax.dot_general(rows, weight_work[:, cols], (((1,), (1,)), ((), ())), pre...  36.3 us
    ppermute x12, starting transfers between devices, from_partner(): lax.ppermute(shard, axis, [(i, i ^ flip) for i in range(lax.axis_size(axi...  21.9 us
    unnamed x18, local copies, waits for them, and re-layouts  14.9 us
  transfers between devices with their start and end apart: 18, of which 14 were waited for; matrix products, arithmetic and copies ran while one was open for 10% of the time, Pallas kernels for 0%

profile of v1, /device:TPU:0, one launch (start us, length us, event | category | flops | bytes accessed | tf_op | source)
XLA Modules:
  0.0 441.0 jit_solution(3005373433382526787)
XLA Ops:
  17.2 6.6 %copy.9 = f32[1,512,3072]{1,2,0:T(8,128)} copy(f32[1,512,3072]{2,1,0:T(8,128)} %param.11) | data formatting | bytes 12582912 | tf_op args[5]
  23.8 3.3 convert_bitcast_fusion
  27.0 35.0 %all-gather.15.cloned.1.call-done = bf16[2048,512]{1,0:T(8,128)(2,1)} async-done(((bf16[128,512]{1,0:T(8,128)(2,1)}), bf16[2048,512]{1,0:T(8,128)(2,1)}) %all-gather.15.cloned.1.call-update) | async-done | bytes 2097168 | tf_op jit(solution)/shard_map/all_gather | solution.py:40
  62.0 4.9 %fusion.17 = f32[2048,512]{1,0:T(8,128)} fusion(bf16[2048,512]{1,0:T(8,128)(2,1)} %all-gather.15.cloned.1.call-done, bf16[512,3072]{1,0:T(8,128)(2,1)S(1)} %convert_bitcast_fusion), kind=kOutput, calls=%fused_computation.46 | convolution fusion | flops 1073741824 | bytes 6815744 | tf_op jit(solution)/shard_map/dot_general | solution.py:48
  66.8 44.7 %all-gather.13.cloned.1.call-done = bf16[2048,512]{1,0:T(8,128)(2,1)} async-done(((bf16[128,512]{1,0:T(8,128)(2,1)}), bf16[2048,512]{1,0:T(8,128)(2,1)}) %all-gather.13.cloned.1.call-update) | async-done | bytes 2097168 | tf_op jit(solution)/shard_map/all_gather | solution.py:40
  111.6 4.9 %fusion.19 = f32[2048,512]{1,0:T(8,128)} fusion(bf16[2048,512]{1,0:T(8,128)(2,1)} %all-gather.13.cloned.1.call-done, bf16[512,3072]{1,0:T(8,128)(2,1)S(1)} %convert_bitcast_fusion), kind=kOutput, calls=%fused_computation.48 | convolution fusion | flops 1073741824 | bytes 6815744 | tf_op jit(solution)/shard_map/dot_general | solution.py:48
  116.5 44.7 %all-gather.11.cloned.1.call-done = bf16[2048,512]{1,0:T(8,128)(2,1)} async-done(((bf16[128,512]{1,0:T(8,128)(2,1)}), bf16[2048,512]{1,0:T(8,128)(2,1)}) %all-gather.11.cloned.1.call-update) | async-done | bytes 2097168 | tf_op jit(solution)/shard_map/all_gather | solution.py:40
  161.2 4.9 %fusion.21 = f32[2048,512]{1,0:T(8,128)} fusion(bf16[2048,512]{1,0:T(8,128)(2,1)} %all-gather.11.cloned.1.call-done, bf16[512,3072]{1,0:T(8,128)(2,1)S(1)} %convert_bitcast_fusion), kind=kOutput, calls=%fused_computation.50 | convolution fusion | flops 1073741824 | bytes 6815744 | tf_op jit(solution)/shard_map/dot_general | solution.py:48
  166.0 44.6 %all-gather.9.cloned.1.call-done = bf16[2048,512]{1,0:T(8,128)(2,1)} async-done(((bf16[128,512]{1,0:T(8,128)(2,1)}), bf16[2048,512]{1,0:T(8,128)(2,1)}) %all-gather.9.cloned.1.call-update) | async-done | bytes 2097168 | tf_op jit(solution)/shard_map/all_gather | solution.py:40
  210.6 4.8 %fusion.23 = f32[2048,512]{1,0:T(8,128)} fusion(bf16[2048,512]{1,0:T(8,128)(2,1)} %all-gather.9.cloned.1.call-done, bf16[512,3072]{1,0:T(8,128)(2,1)S(1)} %convert_bitcast_fusion), kind=kOutput, calls=%fused_computation.52 | convolution fusion | flops 1073741824 | bytes 6815744 | tf_op jit(solution)/shard_map/dot_general | solution.py:48
  215.4 44.6 %all-gather.7.cloned.1.call-done = bf16[2048,512]{1,0:T(8,128)(2,1)} async-done(((bf16[128,512]{1,0:T(8,128)(2,1)}), bf16[2048,512]{1,0:T(8,128)(2,1)}) %all-gather.7.cloned.1.call-update) | async-done | bytes 2097168 | tf_op jit(solution)/shard_map/all_gather | solution.py:40
  260.0 4.9 %fusion.25 = f32[2048,512]{1,0:T(8,128)} fusion(bf16[2048,512]{1,0:T(8,128)(2,1)} %all-gather.7.cloned.1.call-done, bf16[512,3072]{1,0:T(8,128)(2,1)S(1)} %convert_bitcast_fusion), kind=kOutput, calls=%fused_computation.54 | convolution fusion | flops 1073741824 | bytes 6815744 | tf_op jit(solution)/shard_map/dot_general | solution.py:48
  264.9 45.2 %all-gather.17.cloned.1.call-done = bf16[2048,512]{1,0:T(8,128)(2,1)} async-done(((bf16[128,512]{1,0:T(8,128)(2,1)}), bf16[2048,512]{1,0:T(8,128)(2,1)}) %all-gather.17.cloned.1.call-update) | async-done | bytes 2097168 | tf_op jit(solution)/shard_map/all_gather | solution.py:40
  310.0 12.0 %fusion.8 = (bf16[1,2048,512]{2,1,0:T(8,128)(2,1)}, bf16[1,2048,512]{2,1,0:T(8,128)(2,1)}, bf16[2048,512]{1,0:T(8,128)(2,1)S(1)}) fusion(bf16[1,2048,512]{2,1,0:T(8,128)(2,1)} %param.7, bf16[1,2048,512]{2,1,0:T(8,128)(2,1)} %param.8, bf16[2048,512]{1,0:T(8,128)(2,1)} %all-gather.17.cloned.1.call-done, bf16[512,3072]{1,0:T(8,128)(2,1)S(1)} %convert_bitcast_fusion, ...), kind=kOutput, calls=%fused_computation.18 | convolution fusion | flops 1096810496 | bytes 34078720 | tf_op jit(solution)/shard_map/dot_general | solution.py:48
  339.8 9.6 %collective-permute-done.2 = bf16[512,512]{0,1:T(8,128)(2,1)S(1)} collective-permute-done((bf16[512,512]{0,1:T(8,128)(2,1)S(1)}, bf16[512,512]{0,1:T(8,128)(2,1)S(1)}, u32[]{:S(2)}, u32[]{:S(2)}) %collective-permute-start.2) | collective-permute-done | bytes 524320 | tf_op jit(solution)/shard_map/ppermute | solution.py:12
  352.3 8.4 %collective-permute-done.4 = bf16[512,512]{0,1:T(8,128)(2,1)S(1)} collective-permute-done((bf16[512,512]{0,1:T(8,128)(2,1)S(1)}, bf16[512,512]{0,1:T(8,128)(2,1)S(1)}, u32[]{:S(2)}, u32[]{:S(2)}) %collective-permute-start.4) | collective-permute-done | bytes 524320 | tf_op jit(solution)/shard_map/ppermute | solution.py:12
  363.5 8.4 %collective-permute-done.6 = bf16[512,512]{0,1:T(8,128)(2,1)S(1)} collective-permute-done((bf16[512,512]{0,1:T(8,128)(2,1)S(1)}, bf16[512,512]{0,1:T(8,128)(2,1)S(1)}, u32[]{:S(2)}, u32[]{:S(2)}) %collective-permute-start.6) | collective-permute-done | bytes 524320 | tf_op jit(solution)/shard_map/ppermute | solution.py:12
  374.8 8.4 %collective-permute-done.8 = bf16[512,512]{0,1:T(8,128)(2,1)S(1)} collective-permute-done((bf16[512,512]{0,1:T(8,128)(2,1)S(1)}, bf16[512,512]{0,1:T(8,128)(2,1)S(1)}, u32[]{:S(2)}, u32[]{:S(2)}) %collective-permute-start.8) | collective-permute-done | bytes 524320 | tf_op jit(solution)/shard_map/ppermute | solution.py:12
  386.0 7.7 %collective-permute-done.10 = bf16[512,512]{0,1:T(8,128)(2,1)S(1)} collective-permute-done((bf16[512,512]{0,1:T(8,128)(2,1)S(1)}, bf16[512,512]{0,1:T(8,128)(2,1)S(1)}, u32[]{:S(2)}, u32[]{:S(2)}) %collective-permute-start.10) | collective-permute-done | bytes 524320 | tf_op jit(solution)/shard_map/ppermute | solution.py:12
  393.7 2.7 collective-permute-start.9
  398.4 11.4 %collective-permute-done.9 = bf16[512,512]{0,1:T(8,128)(2,1)S(1)} collective-permute-done((bf16[512,512]{0,1:T(8,128)(2,1)S(1)}, bf16[512,512]{0,1:T(8,128)(2,1)S(1)}, u32[]{:S(2)}, u32[]{:S(2)}) %collective-permute-start.9) | collective-permute-done | bytes 524320 | tf_op jit(solution)/shard_map/ppermute | solution.py:12
  410.0 9.4 %collective-permute-done.11 = bf16[512,512]{0,1:T(8,128)(2,1)S(1)} collective-permute-done((bf16[512,512]{0,1:T(8,128)(2,1)S(1)}, bf16[512,512]{0,1:T(8,128)(2,1)S(1)}, u32[]{:S(2)}, u32[]{:S(2)}) %collective-permute-start.11) | collective-permute-done | bytes 524320 | tf_op jit(solution)/shard_map/ppermute | solution.py:12
  423.4 4.2 divide_subtract_fusion
  427.6 6.6 %copy.10 = f32[1,512,3072]{2,1,0:T(8,128)} copy(f32[1,512,3072]{1,2,0:T(8,128)} %divide_subtract_fusion) | data formatting | bytes 12582912
  (75 shorter events, 41.9 us)
Async XLA Ops:
  7.2 54.8 %all-gather.15.cloned.1.call-start = ((), (), s32[]{:S(2)}) async-start(), calls=%async_computation.4 | async-start | bytes 2228224 | tf_op jit(solution)/shard_map/all_gather | solution.py:40
  10.0 101.5 %all-gather.13.cloned.1.call-start = ((), (), s32[]{:S(2)}) async-start(), calls=%async_computation.3 | async-start | bytes 2228224 | tf_op jit(solution)/shard_map/all_gather | solution.py:40
  10.8 150.4 %all-gather.11.cloned.1.call-start = ((), (), s32[]{:S(2)}) async-start(), calls=%async_computation.2 | async-start | bytes 2228224 | tf_op jit(solution)/shard_map/all_gather | solution.py:40
  11.5 199.1 %all-gather.9.cloned.1.call-start = ((), (), s32[]{:S(2)}) async-start(), calls=%async_computation.1 | async-start | bytes 2228224 | tf_op jit(solution)/shard_map/all_gather | solution.py:40
  12.1 247.9 %all-gather.7.cloned.1.call-start = ((), (), s32[]{:S(2)}) async-start(), calls=%async_computation | async-start | bytes 2228224 | tf_op jit(solution)/shard_map/all_gather | solution.py:40
  12.7 297.4 %all-gather.17.cloned.1.call-start = ((), (), s32[]{:S(2)}) async-start(), calls=%async_computation.5 | async-start | bytes 2228224 | tf_op jit(solution)/shard_map/all_gather | solution.py:40
  310.0 12.0 %copy-start.4 = (bf16[2048,512]{1,0:T(8,128)(2,1)S(1)}, bf16[2048,512]{1,0:T(8,128)(2,1)}, u32[]{:S(2)}) copy-start(bf16[2048,512]{1,0:T(8,128)(2,1)} %all-gather.7.cloned.1.call-done) | copy-start | bytes 6291460
  322.1 2.9 copy-start.3
  323.4 3.7 copy-start.2
  323.4 14.8 %collective-permute-start = (bf16[512,512]{0,1:T(8,128)(2,1)S(1)}, bf16[512,512]{0,1:T(8,128)(2,1)S(1)}, u32[]{:S(2)}, u32[]{:S(2)}) collective-permute-start(bf16[512,512]{0,1:T(8,128)(2,1)S(1)} %get-tuple-element.18), channel_id=1, source_target_pairs={{0,16},{16,0},{32,48},{48,32},{64,80},{80,64},{96,112},{112,96},{1... | collective-permute-start | bytes 1572872 | tf_op jit(solution)/shard_map/ppermute | solution.py:12
  326.2 3.7 copy-start.1
  326.3 23.2 %collective-permute-start.2 = (bf16[512,512]{0,1:T(8,128)(2,1)S(1)}, bf16[512,512]{0,1:T(8,128)(2,1)S(1)}, u32[]{:S(2)}, u32[]{:S(2)}) collective-permute-start(bf16[512,512]{0,1:T(8,128)(2,1)S(1)} %get-tuple-element.20), channel_id=1, source_target_pairs={{0,16},{16,0},{32,48},{48,32},{64,80},{80,64},{96,112},{112,96},{1... | collective-permute-start | bytes 1572872 | tf_op jit(solution)/shard_map/ppermute | solution.py:12
  328.4 3.5 copy-start
  328.4 32.3 %collective-permute-start.4 = (bf16[512,512]{0,1:T(8,128)(2,1)S(1)}, bf16[512,512]{0,1:T(8,128)(2,1)S(1)}, u32[]{:S(2)}, u32[]{:S(2)}) collective-permute-start(bf16[512,512]{0,1:T(8,128)(2,1)S(1)} %get-tuple-element.22), channel_id=1, source_target_pairs={{0,16},{16,0},{32,48},{48,32},{64,80},{80,64},{96,112},{112,96},{1... | collective-permute-start | bytes 1572872 | tf_op jit(solution)/shard_map/ppermute | solution.py:12
  331.3 3.5 copy-start.5
  331.3 40.6 %collective-permute-start.6 = (bf16[512,512]{0,1:T(8,128)(2,1)S(1)}, bf16[512,512]{0,1:T(8,128)(2,1)S(1)}, u32[]{:S(2)}, u32[]{:S(2)}) collective-permute-start(bf16[512,512]{0,1:T(8,128)(2,1)S(1)} %get-tuple-element.24), channel_id=1, source_target_pairs={{0,16},{16,0},{32,48},{48,32},{64,80},{80,64},{96,112},{112,96},{1... | collective-permute-start | bytes 1572872 | tf_op jit(solution)/shard_map/ppermute | solution.py:12
  333.2 49.9 %collective-permute-start.8 = (bf16[512,512]{0,1:T(8,128)(2,1)S(1)}, bf16[512,512]{0,1:T(8,128)(2,1)S(1)}, u32[]{:S(2)}, u32[]{:S(2)}) collective-permute-start(bf16[512,512]{0,1:T(8,128)(2,1)S(1)} %get-tuple-element.26), channel_id=1, source_target_pairs={{0,16},{16,0},{32,48},{48,32},{64,80},{80,64},{96,112},{112,96},{1... | collective-permute-start | bytes 1572872 | tf_op jit(solution)/shard_map/ppermute | solution.py:12
  338.2 55.5 %collective-permute-start.10 = (bf16[512,512]{0,1:T(8,128)(2,1)S(1)}, bf16[512,512]{0,1:T(8,128)(2,1)S(1)}, u32[]{:S(2)}, u32[]{:S(2)}) collective-permute-start(bf16[512,512]{0,1:T(8,128)(2,1)S(1)} %get-tuple-element.28), channel_id=1, source_target_pairs={{0,16},{16,0},{32,48},{48,32},{64,80},{80,64},{96,112},{112,96},{1... | collective-permute-start | bytes 1572872 | tf_op jit(solution)/shard_map/ppermute | solution.py:12
  349.5 47.1 %collective-permute-start.1 = (bf16[512,512]{0,1:T(8,128)(2,1)S(1)}, bf16[512,512]{0,1:T(8,128)(2,1)S(1)}, u32[]{:S(2)}, u32[]{:S(2)}) collective-permute-start(bf16[512,512]{0,1:T(8,128)(2,1)S(1)} %fusion.10), channel_id=1, source_target_pairs={{0,48},{16,32},{32,16},{48,0},{64,112},{80,96},{96,80},{112,64},{1... | collective-permute-start | bytes 1572872 | tf_op jit(solution)/shard_map/ppermute | solution.py:12
  360.7 37.0 %collective-permute-start.3 = (bf16[512,512]{0,1:T(8,128)(2,1)S(1)}, bf16[512,512]{0,1:T(8,128)(2,1)S(1)}, u32[]{:S(2)}, u32[]{:S(2)}) collective-permute-start(bf16[512,512]{0,1:T(8,128)(2,1)S(1)} %fusion.11), channel_id=1, source_target_pairs={{0,48},{16,32},{32,16},{48,0},{64,112},{80,96},{96,80},{112,64},{1... | collective-permute-start | bytes 1572872 | tf_op jit(solution)/shard_map/ppermute | solution.py:12
  371.9 26.0 %collective-permute-start.5 = (bf16[512,512]{0,1:T(8,128)(2,1)S(1)}, bf16[512,512]{0,1:T(8,128)(2,1)S(1)}, u32[]{:S(2)}, u32[]{:S(2)}) collective-permute-start(bf16[512,512]{0,1:T(8,128)(2,1)S(1)} %fusion.12), channel_id=1, source_target_pairs={{0,48},{16,32},{32,16},{48,0},{64,112},{80,96},{96,80},{112,64},{1... | collective-permute-start | bytes 1572872 | tf_op jit(solution)/shard_map/ppermute | solution.py:12
  383.2 15.0 %collective-permute-start.7 = (bf16[512,512]{0,1:T(8,128)(2,1)S(1)}, bf16[512,512]{0,1:T(8,128)(2,1)S(1)}, u32[]{:S(2)}, u32[]{:S(2)}) collective-permute-start(bf16[512,512]{0,1:T(8,128)(2,1)S(1)} %fusion.13), channel_id=1, source_target_pairs={{0,48},{16,32},{32,16},{48,0},{64,112},{80,96},{96,80},{112,64},{1... | collective-permute-start | bytes 1572872 | tf_op jit(solution)/shard_map/ppermute | solution.py:12
  393.7 16.1 %collective-permute-start.9 = (bf16[512,512]{0,1:T(8,128)(2,1)S(1)}, bf16[512,512]{0,1:T(8,128)(2,1)S(1)}, u32[]{:S(2)}, u32[]{:S(2)}) collective-permute-start(bf16[512,512]{0,1:T(8,128)(2,1)S(1)} %fusion.14), channel_id=1, source_target_pairs={{0,48},{16,32},{32,16},{48,0},{64,112},{80,96},{96,80},{112,64},{1... | collective-permute-start | bytes 1572872 | tf_op jit(solution)/shard_map/ppermute | solution.py:12
  396.6 22.8 %collective-permute-start.11 = (bf16[512,512]{0,1:T(8,128)(2,1)S(1)}, bf16[512,512]{0,1:T(8,128)(2,1)S(1)}, u32[]{:S(2)}, u32[]{:S(2)}) collective-permute-start(bf16[512,512]{0,1:T(8,128)(2,1)S(1)} %fusion.15), channel_id=1, source_target_pairs={{0,48},{16,32},{32,16},{48,0},{64,112},{80,96},{96,80},{112,64},{1... | collective-permute-start | bytes 1572872 | tf_op jit(solution)/shard_map/ppermute | solution.py:12
  (2 other events, 4.7 us)
Sparse Core Ops, SparseCore 0:
  11.0 50.9 all-gather.14
  64.4 47.0 all-gather.12
  114.0 47.0 all-gather.10
  163.5 47.0 all-gather.8
  212.9 47.0 all-gather.6
  262.9 47.0 all-gather.16

commit v2 on v0

v2 whole, which is shorter than its diff:
```python
import jax
import jax.numpy as jnp
from jax import lax
from jax.experimental import pallas as pl
from jax.experimental.pallas import tpu as pltpu
from jax.sharding import PartitionSpec as P

learn_rate = 0.02
rms_eps = 1e-06
chunk = 256
row_tile = 256
out_tile = 64
MESH = pl.DeviceIdType.MESH


def activations(gate_ref, up_ref, rows):
    gate_val = gate_ref[rows, :].astype(jnp.float32)
    up_val = up_ref[rows, :].astype(jnp.float32)
    return gate_val, up_val, lax.logistic(gate_val)


def kernel(
    grad_hbm, gate_hbm, up_hbm, counts_ref, place_ref, master_hbm,
    dgate_hbm, dup_hbm, new_hbm,
    grad_v, rows_v, gate_v, up_v, hidden_t, d_hidden, weight_v, master_v, total,
    pair_out, pair_in, quad_out, quad_in, squares,
    load_sem, store_sem, gather_send, gather_recv, pair_send, pair_recv, quad_send, quad_recv,
):
    expert, shard = lax.axis_index("expert"), lax.axis_index("shard")
    block, width = grad_v.shape
    n_chunks = width // chunk
    n_rows, n_hidden = gate_v.shape
    half = n_hidden // 2
    n_tiles = n_rows // row_tile

    core = shard % 2
    y = (shard // 2) % 4
    z_base = (shard // 8) * 8
    z_other = (z_base + 8) % 16

    def at(base, step):
        return base + ((y + step + 4) % 4) * 2 + core

    up_id, down_id, far_id = at(z_base, 1), at(z_base, -1), at(z_base, 2)
    across_id = at(z_other, 0)
    sibling_id = shard + 1 - 2 * core
    way = 1 - 2 * core
    pair_id = expert + 1 - 2 * (expert % 2)
    quad_id = expert + 3 - 2 * (expert % 4)

    barrier = pltpu.get_barrier_semaphore()
    for peer in (
        (expert, up_id), (expert, down_id), (expert, across_id), (expert, sibling_id),
        (pair_id, shard), (quad_id, shard),
    ):
        pl.semaphore_signal(barrier, inc=1, device_id=peer, device_id_type=MESH)

    def load(src, dst, index):
        return pltpu.make_async_copy(src, dst, load_sem.at[index])

    quarter = n_rows // 4

    def gate_load(part):
        rows = pl.ds(pl.multiple_of(part * quarter, quarter), quarter)
        return load(gate_hbm.at[rows], gate_v.at[rows], 2 + part)

    def up_load(part):
        rows = pl.ds(pl.multiple_of(part * quarter, quarter), quarter)
        return load(up_hbm.at[rows], up_v.at[rows], 6 + part)

    grad_load = load(grad_hbm, grad_v, 0)
    master_load = load(master_hbm, master_v, 1)
    grad_load.start()
    for part in range(4):
        gate_load(part).start()
        up_load(part).start()
    master_load.start()

    same_pair = jnp.where(place_ref[expert] == place_ref[pair_id], 1.0, 0.0)
    same_quad = jnp.where(place_ref[expert] == place_ref[quad_id], 1.0, 0.0)

    def rows_of(c, b):
        return rows_v.at[c, pl.ds(pl.multiple_of(b * block, block), block)]

    def some_blocks(c, n):
        return rows_v.at[c, pl.ds(0, n * block)]

    def push(c, b, target, stage):
        pltpu.make_async_remote_copy(
            src_ref=rows_of(c, b),
            dst_ref=rows_of(c, b),
            send_sem=gather_send.at[c],
            recv_sem=gather_recv.at[c, stage],
            device_id=(expert, target),
            device_id_type=MESH,
        ).start()

    def arrived(c, stage, n):
        pltpu.make_async_copy(
            some_blocks(c, n), some_blocks(c, n), gather_recv.at[c, stage]
        ).wait()

    def exchange(out, landing, send_sem, recv_sem, target, c, h):
        return pltpu.make_async_remote_copy(
            src_ref=out.at[c, h],
            dst_ref=landing.at[c, h],
            send_sem=send_sem.at[c, h],
            recv_sem=recv_sem.at[c, h],
            device_id=(target, shard),
            device_id_type=MESH,
        )

    def pair_copy(c, h):
        return exchange(pair_out, pair_in, pair_send, pair_recv, pair_id, c, h)

    def quad_copy(c, h):
        return exchange(quad_out, quad_in, quad_send, quad_recv, quad_id, c, h)

    def columns(c):
        return pl.ds(pl.multiple_of(c * chunk, chunk), chunk)

    grad_load.wait()
    live = lax.broadcasted_iota(jnp.int32, (block, chunk), 0) < counts_ref[0, 0]
    own_rows = pl.ds(pl.multiple_of(shard * block, block), block)

    @pl.loop(0, n_chunks)
    def _(c):
        values = grad_v[:, columns(c)].astype(jnp.float32)
        rows_v[c, own_rows, :] = jnp.where(live, values, 0.0).astype(jnp.bfloat16)

    pl.semaphore_wait(barrier, 6)

    def make_hidden(tile):
        rows = pl.ds(pl.multiple_of(tile * row_tile, row_tile), row_tile)
        gate_val, up_val, sig = activations(gate_v, up_v, rows)
        hidden_t[:, rows] = jnp.transpose(gate_val * sig * up_val).astype(jnp.bfloat16)

    def finish_rows(tile):
        rows = pl.ds(pl.multiple_of(tile * row_tile, row_tile), row_tile)
        gate_val, up_val, sig = activations(gate_v, up_v, rows)
        grad = d_hidden[rows, :]
        up_v[rows, :] = (grad * (gate_val * sig)).astype(jnp.bfloat16)
        slope = sig * (1.0 + gate_val * (1.0 - sig))
        gate_v[rows, :] = (grad * up_val * slope).astype(jnp.bfloat16)
        pltpu.make_async_copy(gate_v.at[rows], dgate_hbm.at[rows], store_sem.at[0, tile]).start()
        pltpu.make_async_copy(up_v.at[rows], dup_hbm.at[rows], store_sem.at[1, tile]).start()

    def step(t, carry):
        @pl.when(t < n_chunks)
        def _():
            for target in (up_id, down_id, across_id):
                push(t, shard, target, 0)
            push(t, shard, sibling_id, 3)

        @pl.when(jnp.logical_and(t >= 1, t < n_chunks + 1))
        def _():
            c = t - 1
            arrived(c, 0, 3)
            push(c, across_id, up_id, 1)
            push(c, across_id, down_id, 1)
            push(c, at(z_base, -way), at(z_base, way), 1)
            for b in (across_id, up_id, down_id):
                push(c, b, sibling_id, 3)

        @pl.when(jnp.logical_and(t >= 2, t < n_chunks + 2))
        def _():
            c = t - 2
            arrived(c, 1, 3)
            push(c, far_id, across_id, 2)
            for b in (far_id, at(z_other, 1), at(z_other, -1)):
                push(c, b, sibling_id, 3)

        @pl.when(jnp.logical_and(t >= 3, t < n_chunks + 3))
        def _():
            c = t - 3
            arrived(c, 2, 1)
            push(c, at(z_other, 2), sibling_id, 3)

        @pl.when(t < 4)
        def _():
            gate_load(t).wait()
            up_load(t).wait()
            for k in range(2):
                make_hidden(2 * t + k)

        @pl.when(t == 3)
        def _():
            master_load.wait()
            d_hidden[...] = jnp.zeros_like(d_hidden)
            squares[...] = jnp.zeros_like(squares)

        @pl.when(jnp.logical_and(t >= 4, t < n_chunks + 4))
        def _():
            c = t - 4
            arrived(c, 3, 8)
            for h in range(2):
                part = pl.ds(h * half, half)
                grad = jnp.dot(
                    hidden_t[part, :], rows_v[c], preferred_element_type=jnp.float32
                )
                total[part, columns(c)] = grad
                pair_out[c, h] = grad.astype(jnp.bfloat16)
                pair_copy(c, h).start()
            weight_v[...] = master_v[:, columns(c)].astype(jnp.bfloat16)

            @pl.loop(0, n_tiles)
            def _(tile):
                rows = pl.ds(pl.multiple_of(tile * row_tile, row_tile), row_tile)
                d_hidden[rows, :] += lax.dot_general(
                    rows_v[c, rows, :], weight_v[...], (((1,), (1,)), ((), ())),
                    preferred_element_type=jnp.float32,
                )

        @pl.when(jnp.logical_and(t >= 5, t < n_chunks + 5))
        def _():
            c = t - 5
            for h in range(2):
                part = pl.ds(h * half, half)
                pair_copy(c, h).wait_recv()
                both = total[part, columns(c)] + same_pair * pair_in[c, h].astype(jnp.float32)
                total[part, columns(c)] = both
                quad_out[c, h] = both.astype(jnp.bfloat16)
                quad_copy(c, h).start()

        @pl.when(jnp.logical_and(t >= n_chunks + 3, t < n_chunks + 5))
        def _():
            @pl.loop(0, n_tiles // 2)
            def _(k):
                finish_rows((t - n_chunks - 3) * (n_tiles // 2) + k)

        @pl.when(t >= 7)
        def _():
            c = t - 7
            for h in range(2):
                part = pl.ds(h * half, half)
                quad_copy(c, h).wait_recv()
                whole = total[part, columns(c)] + same_quad * quad_in[c, h].astype(jnp.float32)
                total[part, columns(c)] = whole
                square = whole * whole
                squares[part, :] += square[:, :128] + square[:, 128:]

        return carry

    lax.fori_loop(0, n_chunks + 7, step, 0)

    def new_store(tile):
        rows = pl.ds(pl.multiple_of(tile * out_tile, out_tile), out_tile)
        return pltpu.make_async_copy(master_v.at[rows], new_hbm.at[rows], store_sem.at[2, tile])

    @pl.loop(0, n_hidden // out_tile)
    def _(tile):
        rows = pl.ds(pl.multiple_of(tile * out_tile, out_tile), out_tile)
        mean = jnp.sum(squares[rows, :], axis=1, keepdims=True) / width
        scale = learn_rate / jnp.sqrt(mean + rms_eps)
        master_v[rows, :] = master_v[rows, :] - total[rows, :] * scale
        new_store(tile).start()

    @pl.loop(0, n_chunks)
    def _(c):
        pltpu.make_async_copy(some_blocks(c, 15), some_blocks(c, 15), gather_send.at[c]).wait()
        for h in range(2):
            pair_copy(c, h).wait_send()
            quad_copy(c, h).wait_send()

    @pl.loop(0, n_tiles)
    def _(tile):
        rows = pl.ds(pl.multiple_of(tile * row_tile, row_tile), row_tile)
        pltpu.make_async_copy(gate_v.at[rows], dgate_hbm.at[rows], store_sem.at[0, tile]).wait()
        pltpu.make_async_copy(up_v.at[rows], dup_hbm.at[rows], store_sem.at[1, tile]).wait()

    @pl.loop(0, n_hidden // out_tile)
    def _(tile):
        new_store(tile).wait()


def per_device(grad_out, gate_pre, up_pre, counts, placement, master):
    block, width = grad_out.shape[1:]
    n_rows, n_hidden = gate_pre.shape[1:]
    n_chunks = width // chunk
    half = n_hidden // 2
    hbm = pl.BlockSpec(memory_space=pl.ANY)
    smem = pl.BlockSpec(memory_space=pltpu.SMEM)
    dma = pltpu.SemaphoreType.DMA
    pieces = (n_chunks, 2, half, chunk)
    d_gate, d_up, new_master = pl.pallas_call(
        kernel,
        out_shape=(
            jax.ShapeDtypeStruct((n_rows, n_hidden), jnp.bfloat16),
            jax.ShapeDtypeStruct((n_rows, n_hidden), jnp.bfloat16),
            jax.ShapeDtypeStruct((n_hidden, width), jnp.float32),
        ),
        in_specs=[hbm, hbm, hbm, smem, smem, hbm],
        out_specs=(hbm, hbm, hbm),
        scratch_shapes=[
            pltpu.VMEM((block, width), jnp.bfloat16),
            pltpu.VMEM((n_chunks, n_rows, chunk), jnp.bfloat16),
            pltpu.VMEM((n_rows, n_hidden), jnp.bfloat16),
            pltpu.VMEM((n_rows, n_hidden), jnp.bfloat16),
            pltpu.VMEM((n_hidden, n_rows), jnp.bfloat16),
            pltpu.VMEM((n_rows, n_hidden), jnp.float32),
            pltpu.VMEM((n_hidden, chunk), jnp.bfloat16),
            pltpu.VMEM((n_hidden, width), jnp.float32),
            pltpu.VMEM((n_hidden, width), jnp.float32),
            pltpu.VMEM(pieces, jnp.bfloat16),
            pltpu.VMEM(pieces, jnp.bfloat16),
            pltpu.VMEM(pieces, jnp.bfloat16),
            pltpu.VMEM(pieces, jnp.bfloat16),
            pltpu.VMEM((n_hidden, 128), jnp.float32),
            dma((10,)),
            dma((3, 8)),
            dma((n_chunks,)),
            dma((n_chunks, 4)),
            dma((n_chunks, 2)),
            dma((n_chunks, 2)),
            dma((n_chunks, 2)),
            dma((n_chunks, 2)),
        ],
        compiler_params=pltpu.CompilerParams(
            collective_id=0, has_side_effects=True, vmem_limit_bytes=58 * 2**20
        ),
    )(grad_out[0], gate_pre[0], up_pre[0], counts, placement, master[0])
    return d_gate[None], d_up[None], new_master[None]


def solution(mesh):
    return jax.shard_map(
        per_device,
        mesh=mesh,
        in_specs=(
            P("expert", "shard", None),
            P("expert", None, "shard"),
            P("expert", None, "shard"),
            P("expert", "shard"),
            P(),
            P("expert", "shard", None),
        ),
        out_specs=(
            P("expert", None, "shard"),
            P("expert", None, "shard"),
            P("expert", "shard", None),
        ),
        check_vma=False,
    )
```

time: 285 us -> 114 us (0.40)
  waiting for transfers between devices: 212 us -> 0 us
  Pallas kernels: 0 us -> 104 us
  matrix products: 30 us -> 0 us
  other arithmetic: 19.6 us -> 0 us
  between operations: 17.4 us -> 1.29 us
  local copies, waits for them, and re-layouts: 1.67 us -> 8.95 us
  starting transfers between devices: 4.49 us -> 0 us
    ppermute x2 -> x0, waiting for transfers between devices: 117 us -> none  [from_partner(): lax.ppermute(shard, axis, [(i, i ^ 1 << bit) for i in range(lax.axis_size...]
    pallas_call x0 -> x1, Pallas kernels: none -> 104 us  [per_device(): pl.pallas_call(kernel, out_shape=(jax.ShapeDtypeStruct((n_rows, n_hidden)...]
    all_gather x1 -> x0, waiting for transfers between devices: 94.5 us -> none  [per_device(): block_rows = lax.all_gather(masked, 'shard', axis=0, tiled=True)]
    dot_general x2 -> x0, matrix products: 30 us -> none  [the longest x1 16.6 us: per_device(): lax.dot_general(block_rows, weight_work, (((1,), (1,)), ((), ())), prefer...]
    unnamed x10 -> x5, local copies, waits for them, and re-layouts: 1.67 us -> 8.95 us
    convert_element_type x2 -> x0, other arithmetic: 6.56 us -> none  [the longest x1 6.56 us: per_device(): grad_sum.astype(jnp.bfloat16)]
    broadcast_in_dim x1 -> x0, other arithmetic: 6.48 us -> none  [per_device(): return (gate_acc[None], up_acc[None], new_master[None])]
    ppermute x2 -> x0, starting transfers between devices: 4.45 us -> none  [from_partner(): lax.ppermute(shard, axis, [(i, i ^ 1 << bit) for i in range(lax.axis_size...]
  transfers between devices with their start and end apart: 3 -> 0, of which waited for: 3 -> 0; matrix products, arithmetic and copies ran while one was open for 6% -> 0% of each run, Pallas kernels for 0% -> 0%
where the time goes in v2:
time: 114 us
  Pallas kernels  104 us (91%)
  local copies, waits for them, and re-layouts  8.95 us (8%)
  between operations  1.29 us (1%)
    pallas_call x1, Pallas kernels, per_device(): pl.pallas_call(kernel, out_shape=(jax.ShapeDtypeStruct((n_rows, n_hidden)...  104 us
    unnamed x5, local copies, waits for them, and re-layouts  8.95 us

profile of v2, /device:TPU:0, one launch (start us, length us, event | category | flops | bytes accessed | tf_op | source)
XLA Modules:
  0.0 113.8 jit_solution(313110220345529839)
XLA Ops:
  1.3 103.6 %shard_map.85 = (bf16[2048,512]{1,0:T(8,128)(2,1)}, bf16[2048,512]{1,0:T(8,128)(2,1)}, f32[512,3072]{1,0:T(8,128)}) custom-call(bf16[128,3072]{1,0:T(8,128)(2,1)} %bitcast.13, bf16[2048,512]{1,0:T(8,128)(2,1)} %bitcast.11, bf16[2048,512]{1,0:T(8,128)(2,1)} %bitcast.12, s32[1,1]{1,0:T(1,128)S(6)} %copy.12.counts_ref, s32[8]{0:T(128)} %place_ref.1, ...), custom_call_target="tpu_custom_call" | custom-call | tf_op jit(solution)/shard_map/pallas_call | solution.py:285
  104.8 0.0 copy-start
  104.9 3.2 %copy.13 = bf16[1,2048,512]{2,1,0:T(8,128)(2,1)} copy(bf16[1,2048,512]{2,1,0:T(8,128)(2,1)} %bitcast.10) | data formatting | bytes 4194304
  108.1 3.0 %copy.14 = bf16[1,2048,512]{2,1,0:T(8,128)(2,1)} copy(bf16[1,2048,512]{2,1,0:T(8,128)(2,1)} %bitcast.9) | data formatting | bytes 4194304
  111.1 0.0 copy-done
  111.1 2.7 %copy.15 = f32[1,512,3072]{2,1,0:T(8,128)} copy(f32[1,512,3072]{2,1,0:T(8,128)S(1)} %bitcast.8) | data formatting | bytes 12582912
Async XLA Ops:
  104.8 6.3 %copy-start = (f32[512,3072]{1,0:T(8,128)S(1)}, f32[512,3072]{1,0:T(8,128)}, u32[]{:S(2)}) copy-start(f32[512,3072]{1,0:T(8,128)} %get-tuple-element.8) | copy-start | bytes 18874372

commit v3 on v0

v3 whole, which is shorter than its diff:
```python
import jax
import jax.numpy as jnp
from jax import lax
from jax.experimental import pallas as pl
from jax.experimental.pallas import tpu as pltpu
from jax.sharding import PartitionSpec as P

learn_rate = 0.02
rms_eps = 1e-06
piece = 128
chunk = 256
row_tile = 256
out_tile = 64
MESH = pl.DeviceIdType.MESH


def activations(gate_ref, up_ref, rows):
    gate_val = gate_ref[rows, :].astype(jnp.float32)
    up_val = up_ref[rows, :].astype(jnp.float32)
    return gate_val, up_val, lax.logistic(gate_val)


def kernel(
    grad_hbm, gate_hbm, up_hbm, counts_ref, place_ref, master_hbm,
    gate_v, up_v, master_v, total, squares,
    grad_v, rows_v, hidden_t, d_hidden, weight_t,
    pair_out, pair_in, quad_out, quad_in,
    load_sem, gather_send, gather_recv, pair_send, pair_recv, quad_send, quad_recv,
):
    expert, shard = lax.axis_index("expert"), lax.axis_index("shard")
    block, width = grad_v.shape
    n_pieces = width // piece
    n_units = n_pieces // 2 + 1
    n_rows, n_hidden = gate_v.shape
    n_tiles = n_rows // row_tile

    core = shard % 2
    y = (shard // 2) % 4
    z_base = (shard // 8) * 8
    z_other = (z_base + 8) % 16

    def at(base, step):
        return base + ((y + step + 4) % 4) * 2 + core

    up_id, down_id, far_id = at(z_base, 1), at(z_base, -1), at(z_base, 2)
    across_id = at(z_other, 0)
    sibling_id = shard + 1 - 2 * core
    way = 1 - 2 * core
    pair_id = expert + 1 - 2 * (expert % 2)
    quad_id = expert + 3 - 2 * (expert % 4)

    barrier = pltpu.get_barrier_semaphore()
    for peer in (
        (expert, up_id), (expert, down_id), (expert, across_id), (expert, sibling_id),
        (pair_id, shard), (quad_id, shard),
    ):
        pl.semaphore_signal(barrier, inc=1, device_id=peer, device_id_type=MESH)

    def load(src, dst, index):
        return pltpu.make_async_copy(src, dst, load_sem.at[index])

    quarter = n_rows // 4

    def gate_load(part):
        rows = pl.ds(pl.multiple_of(part * quarter, quarter), quarter)
        return load(gate_hbm.at[rows], gate_v.at[rows], 3 + part)

    def up_load(part):
        rows = pl.ds(pl.multiple_of(part * quarter, quarter), quarter)
        return load(up_hbm.at[rows], up_v.at[rows], 7 + part)

    first, rest = pl.ds(0, chunk), pl.ds(chunk, width - chunk)
    first_load = load(grad_hbm.at[:, first], grad_v.at[:, first], 0)
    rest_load = load(grad_hbm.at[:, rest], grad_v.at[:, rest], 1)
    master_load = load(master_hbm, master_v, 2)
    first_load.start()
    for part in range(4):
        gate_load(part).start()
        up_load(part).start()
    rest_load.start()
    master_load.start()

    same_pair = jnp.where(place_ref[expert] == place_ref[pair_id], 1.0, 0.0)
    same_quad = jnp.where(place_ref[expert] == place_ref[quad_id], 1.0, 0.0)

    def block_of(p, n, b):
        return rows_v.at[pl.ds(p, n), pl.ds(pl.multiple_of(b * block, block), block)]

    def some_blocks(n, k):
        return rows_v.at[pl.ds(0, n), pl.ds(0, k * block)]

    def per_unit(u, act):
        @pl.when(u < 2)
        def _():
            act(u, 1)

        @pl.when(u >= 2)
        def _():
            act(2 * u - 2, 2)

    def push(u, p, n, b, target, stage):
        pltpu.make_async_remote_copy(
            src_ref=block_of(p, n, b),
            dst_ref=block_of(p, n, b),
            send_sem=gather_send.at[u],
            recv_sem=gather_recv.at[u, stage],
            device_id=(expert, target),
            device_id_type=MESH,
        ).start()

    def arrived(u, n, stage, k):
        blocks = some_blocks(n, k)
        pltpu.make_async_copy(blocks, blocks, gather_recv.at[u, stage]).wait()

    def exchange(out, landing, send_sem, recv_sem, target, p):
        return pltpu.make_async_remote_copy(
            src_ref=out.at[p],
            dst_ref=landing.at[p],
            send_sem=send_sem.at[p],
            recv_sem=recv_sem.at[p],
            device_id=(target, shard),
            device_id_type=MESH,
        )

    def pair_copy(p):
        return exchange(pair_out, pair_in, pair_send, pair_recv, pair_id, p)

    def quad_copy(p):
        return exchange(quad_out, quad_in, quad_send, quad_recv, quad_id, p)

    def columns(p, n):
        return pl.ds(pl.multiple_of(p * piece, piece), n * piece)

    def rows_of(p, n):
        if n == 1:
            return rows_v[p]
        return jnp.concatenate([rows_v[p], rows_v[p + 1]], axis=1)

    live = lax.broadcasted_iota(jnp.int32, (block, piece), 0) < counts_ref[0, 0]
    own_rows = pl.ds(pl.multiple_of(shard * block, block), block)

    def mask_piece(p):
        values = grad_v[:, columns(p, 1)].astype(jnp.float32)
        rows_v[p, own_rows, :] = jnp.where(live, values, 0.0).astype(jnp.bfloat16)

    first_load.wait()
    mask_piece(0)
    mask_piece(1)
    pl.semaphore_wait(barrier, 6)

    def make_hidden(tile):
        rows = pl.ds(pl.multiple_of(tile * row_tile, row_tile), row_tile)
        gate_val, up_val, sig = activations(gate_v, up_v, rows)
        hidden_t[:, rows] = jnp.transpose(gate_val * sig * up_val).astype(jnp.bfloat16)

    def finish_rows(tile):
        rows = pl.ds(pl.multiple_of(tile * row_tile, row_tile), row_tile)
        gate_val, up_val, sig = activations(gate_v, up_v, rows)
        grad = d_hidden[rows, :]
        up_v[rows, :] = (grad * (gate_val * sig)).astype(jnp.bfloat16)
        slope = sig * (1.0 + gate_val * (1.0 - sig))
        gate_v[rows, :] = (grad * up_val * slope).astype(jnp.bfloat16)

    def during(t, delay, body):
        @pl.when(jnp.logical_and(t >= delay, t < n_units + delay))
        def _():
            body(t - delay)

    def step(t, carry):
        def weight_grad(u):
            def act(p, n):
                arrived(u, n, 3, 8)
                grad = jnp.dot(hidden_t[...], rows_of(p, n), preferred_element_type=jnp.float32)
                total[:, columns(p, n)] = grad
                for k in range(n):
                    pair_out[p + k] = grad[:, k * piece : (k + 1) * piece].astype(jnp.bfloat16)
                    pair_copy(p + k).start()

            per_unit(u, act)

        def stage_three(u):
            def act(p, n):
                arrived(u, n, 2, 1)
                push(u, p, n, at(z_other, 2), sibling_id, 3)

            per_unit(u, act)

        def stage_two(u):
            def act(p, n):
                arrived(u, n, 1, 3)
                push(u, p, n, far_id, across_id, 2)
                for b in (far_id, at(z_other, 1), at(z_other, -1)):
                    push(u, p, n, b, sibling_id, 3)

            per_unit(u, act)

        def stage_one(u):
            def act(p, n):
                arrived(u, n, 0, 3)
                push(u, p, n, across_id, up_id, 1)
                push(u, p, n, across_id, down_id, 1)
                push(u, p, n, at(z_base, -way), at(z_base, way), 1)
                for b in (across_id, up_id, down_id):
                    push(u, p, n, b, sibling_id, 3)

            per_unit(u, act)

        def stage_zero(u):
            def act(p, n):
                for target in (across_id, up_id, down_id):
                    push(u, p, n, shard, target, 0)
                push(u, p, n, shard, sibling_id, 3)

            per_unit(u, act)

        def data_grad(u):
            @pl.when(u >= 1)
            def _():
                p = 2 * u - 2
                weight_t[...] = jnp.transpose(master_v[:, columns(p, 2)]).astype(jnp.bfloat16)
                d_hidden[...] += jnp.dot(
                    rows_of(p, 2), weight_t[...], preferred_element_type=jnp.float32
                )

        def pair_sum(u):
            def act(p, n):
                for k in range(n):
                    pair_copy(p + k).wait_recv()
                    part = columns(p + k, 1)
                    both = total[:, part] + same_pair * pair_in[p + k].astype(jnp.float32)
                    total[:, part] = both
                    quad_out[p + k] = both.astype(jnp.bfloat16)
                    quad_copy(p + k).start()

            per_unit(u, act)

        def quad_sum(u):
            def act(p, n):
                for k in range(n):
                    quad_copy(p + k).wait_recv()
                    part = columns(p + k, 1)
                    whole = total[:, part] + same_quad * quad_in[p + k].astype(jnp.float32)
                    total[:, part] = whole
                    squares[...] += whole * whole

            per_unit(u, act)

        during(t, 4, weight_grad)
        during(t, 3, stage_three)
        during(t, 2, stage_two)
        during(t, 1, stage_one)
        during(t, 0, stage_zero)

        @pl.when(t < 4)
        def _():
            gate_load(t).wait()
            up_load(t).wait()
            for k in range(2):
                make_hidden(2 * t + k)

        @pl.when(t == 1)
        def _():
            rest_load.wait()

            @pl.loop(2, n_pieces)
            def _(p):
                mask_piece(p)

        @pl.when(t == 4)
        def _():
            master_load.wait()
            d_hidden[...] = jnp.zeros_like(d_hidden)
            squares[...] = jnp.zeros_like(squares)

        during(t, 4, data_grad)
        during(t, 5, pair_sum)

        @pl.when(jnp.logical_and(t >= n_units + 3, t < n_units + 5))
        def _():
            @pl.loop(0, n_tiles // 2)
            def _(k):
                finish_rows((t - n_units - 3) * (n_tiles // 2) + k)

        during(t, 7, quad_sum)
        return carry

    lax.fori_loop(0, n_units + 7, step, 0)

    @pl.loop(0, n_units)
    def _(u):
        def act(p, n):
            blocks = some_blocks(n, 15)
            pltpu.make_async_copy(blocks, blocks, gather_send.at[u]).wait()
            for k in range(n):
                pair_copy(p + k).wait_send()
                quad_copy(p + k).wait_send()

        per_unit(u, act)


def finish(
    gate_v, up_v, master_v, total, squares, dgate_hbm, dup_hbm, new_hbm, new_v, store_sem
):
    n_rows, (n_hidden, width) = gate_v.shape[0], master_v.shape
    parts = 4
    copies = []
    for index, (src, dst) in enumerate(((gate_v, dgate_hbm), (up_v, dup_hbm))):
        for part in range(parts):
            rows = pl.ds(part * (n_rows // parts), n_rows // parts)
            copies.append(
                pltpu.make_async_copy(src.at[rows], dst.at[rows], store_sem.at[index, part])
            )

    def new_store(tile):
        rows = pl.ds(pl.multiple_of(tile * out_tile, out_tile), out_tile)
        return pltpu.make_async_copy(new_v.at[rows], new_hbm.at[rows], store_sem.at[2, tile])

    for copy in copies:
        copy.start()

    @pl.loop(0, n_hidden // out_tile)
    def _(tile):
        rows = pl.ds(pl.multiple_of(tile * out_tile, out_tile), out_tile)
        mean = jnp.sum(squares[rows, :], axis=1, keepdims=True) / width
        scale = learn_rate / jnp.sqrt(mean + rms_eps)
        new_v[rows, :] = master_v[rows, :] - total[rows, :] * scale
        new_store(tile).start()

    for copy in copies:
        copy.wait()

    @pl.loop(0, n_hidden // out_tile)
    def _(tile):
        new_store(tile).wait()


def per_device(grad_out, gate_pre, up_pre, counts, placement, master):
    block, width = grad_out.shape[1:]
    n_rows, n_hidden = gate_pre.shape[1:]
    n_pieces = width // piece
    n_units = n_pieces // 2 + 1
    hbm = pl.BlockSpec(memory_space=pl.ANY)
    smem = pl.BlockSpec(memory_space=pltpu.SMEM)
    vmem = pl.BlockSpec(memory_space=pltpu.VMEM)
    dma = pltpu.SemaphoreType.DMA
    pieces = (n_pieces, n_hidden, piece)
    held = pl.pallas_call(
        kernel,
        out_shape=(
            pltpu.VMEM((n_rows, n_hidden), jnp.bfloat16),
            pltpu.VMEM((n_rows, n_hidden), jnp.bfloat16),
            pltpu.VMEM((n_hidden, width), jnp.float32),
            pltpu.VMEM((n_hidden, width), jnp.float32),
            pltpu.VMEM((n_hidden, piece), jnp.float32),
        ),
        in_specs=[hbm, hbm, hbm, smem, smem, hbm],
        out_specs=(vmem,) * 5,
        scratch_shapes=[
            pltpu.VMEM((block, width), jnp.bfloat16),
            pltpu.VMEM((n_pieces, n_rows, piece), jnp.bfloat16),
            pltpu.VMEM((n_hidden, n_rows), jnp.bfloat16),
            pltpu.VMEM((n_rows, n_hidden), jnp.float32),
            pltpu.VMEM((chunk, n_hidden), jnp.bfloat16),
            pltpu.VMEM(pieces, jnp.bfloat16),
            pltpu.VMEM(pieces, jnp.bfloat16),
            pltpu.VMEM(pieces, jnp.bfloat16),
            pltpu.VMEM(pieces, jnp.bfloat16),
            dma((11,)),
            dma((n_units,)),
            dma((n_units, 4)),
            dma((n_pieces,)),
            dma((n_pieces,)),
            dma((n_pieces,)),
            dma((n_pieces,)),
        ],
        compiler_params=pltpu.CompilerParams(
            collective_id=0, has_side_effects=True, vmem_limit_bytes=40 * 2**20
        ),
    )(grad_out[0], gate_pre[0], up_pre[0], counts, placement, master[0])
    d_gate, d_up, new_master = pl.pallas_call(
        finish,
        out_shape=(
            jax.ShapeDtypeStruct((n_rows, n_hidden), jnp.bfloat16),
            jax.ShapeDtypeStruct((n_rows, n_hidden), jnp.bfloat16),
            jax.ShapeDtypeStruct((n_hidden, width), jnp.float32),
        ),
        in_specs=[vmem] * 5,
        out_specs=(hbm,) * 3,
        scratch_shapes=[pltpu.VMEM((n_hidden, width), jnp.float32), dma((3, 8))],
        compiler_params=pltpu.CompilerParams(vmem_limit_bytes=20 * 2**20),
    )(*held)
    return d_gate[None], d_up[None], new_master[None]


def solution(mesh):
    return jax.shard_map(
        per_device,
        mesh=mesh,
        in_specs=(
            P("expert", "shard", None),
            P("expert", None, "shard"),
            P("expert", None, "shard"),
            P("expert", "shard"),
            P(),
            P("expert", "shard", None),
        ),
        out_specs=(
            P("expert", None, "shard"),
            P("expert", None, "shard"),
            P("expert", "shard", None),
        ),
        check_vma=False,
    )
```

time: 285 us -> 116 us (0.41)
  waiting for transfers between devices: 212 us -> 0 us
  Pallas kernels: 0 us -> 115 us
  matrix products: 30 us -> 0 us
  other arithmetic: 19.6 us -> 0 us
  between operations: 17.4 us -> 1.29 us
  starting transfers between devices: 4.49 us -> 0 us
    ppermute x2 -> x0, waiting for transfers between devices: 117 us -> none  [from_partner(): lax.ppermute(shard, axis, [(i, i ^ 1 << bit) for i in range(lax.axis_size...]
    pallas_call x0 -> x2, Pallas kernels: none -> 115 us  [the longest x1 110 us: per_device(): pl.pallas_call(kernel, out_shape=(pltpu.VMEM((n_rows, n_hidden), jnp.bflo...]
    all_gather x1 -> x0, waiting for transfers between devices: 94.5 us -> none  [per_device(): block_rows = lax.all_gather(masked, 'shard', axis=0, tiled=True)]
    dot_general x2 -> x0, matrix products: 30 us -> none  [the longest x1 16.6 us: per_device(): lax.dot_general(block_rows, weight_work, (((1,), (1,)), ((), ())), prefer...]
    convert_element_type x2 -> x0, other arithmetic: 6.56 us -> none  [the longest x1 6.56 us: per_device(): grad_sum.astype(jnp.bfloat16)]
    broadcast_in_dim x1 -> x0, other arithmetic: 6.48 us -> none  [per_device(): return (gate_acc[None], up_acc[None], new_master[None])]
    ppermute x2 -> x0, starting transfers between devices: 4.45 us -> none  [from_partner(): lax.ppermute(shard, axis, [(i, i ^ 1 << bit) for i in range(lax.axis_size...]
    reduce_sum x2 -> x0, other arithmetic: 4.38 us -> none  [the longest x1 3.63 us: per_device(): jnp.mean(grad_sum * grad_sum, axis=1, keepdims=True) + rms_eps]
  transfers between devices with their start and end apart: 3 -> 0, of which waited for: 3 -> 0; matrix products, arithmetic and copies ran while one was open for 6% -> 0% of each run, Pallas kernels for 0% -> 0%
where the time goes in v3:
time: 116 us
  Pallas kernels  115 us (99%)
  between operations  1.29 us (1%)
    pallas_call x1, Pallas kernels, per_device(): pl.pallas_call(kernel, out_shape=(pltpu.VMEM((n_rows, n_hidden), jnp.bflo...  110 us
    pallas_call x1, Pallas kernels, per_device(): pl.pallas_call(finish, out_shape=(jax.ShapeDtypeStruct((n_rows, n_hidden)...  4.13 us

profile of v3, /device:TPU:0, one launch (start us, length us, event | category | flops | bytes accessed | tf_op | source)
XLA Modules:
  0.0 115.8 jit_solution(3582614999472553808)
XLA Ops:
  1.3 110.4 %shard_map.85 = (bf16[2048,512]{1,0:T(8,128)(2,1)S(1)}, bf16[2048,512]{1,0:T(8,128)(2,1)S(1)}, f32[512,3072]{1,0:T(8,128)S(1)}, f32[512,3072]{1,0:T(8,128)S(1)}, f32[512,128]{1,0:T(8,128)S(1)}) custom-call(bf16[128,3072]{1,0:T(8,128)(2,1)} %bitcast.10, bf16[2048,512]{1,0:T(8,128)(2,1)} %bitcast.8, bf16[2048,512]{1,0:T(8,128)(2,1)} %bitcast.9, ...), custom_call_target="tpu_custom_call" | custom-call | tf_op jit(solution)/shard_map/pallas_call | solution.py:347
  111.7 4.1 %shard_map.86 = (bf16[2048,512]{1,0:T(8,128)(2,1)}, bf16[2048,512]{1,0:T(8,128)(2,1)}, f32[512,3072]{1,0:T(8,128)}) custom-call(bf16[2048,512]{1,0:T(8,128)(2,1)S(1)} %get-tuple-element.11.gate_v, bf16[2048,512]{1,0:T(8,128)(2,1)S(1)} %get-tuple-element.12.up_v, f32[512,3072]{1,0:T(8,128)S(1)} %get-tuple-element.13.master_v, ...), custom_call_target="tpu_custom_call" | custom-call | tf_op jit(solution)/shard_map/pallas_call | solution.py:380

commit v4 on v3

--- a/solution.py
+++ b/solution.py
@@ -51,8 +51,8 @@
 
     barrier = pltpu.get_barrier_semaphore()
     for peer in (
-        (expert, up_id), (expert, down_id), (expert, across_id), (expert, sibling_id),
-        (pair_id, shard), (quad_id, shard),
+        (expert, up_id), (expert, down_id), (expert, far_id), (expert, across_id),
+        (expert, sibling_id), (pair_id, shard), (quad_id, shard),
     ):
         pl.semaphore_signal(barrier, inc=1, device_id=peer, device_id_type=MESH)
 
@@ -146,12 +146,18 @@
     first_load.wait()
     mask_piece(0)
     mask_piece(1)
-    pl.semaphore_wait(barrier, 6)
+    pl.semaphore_wait(barrier, 7)
 
     def make_hidden(tile):
         rows = pl.ds(pl.multiple_of(tile * row_tile, row_tile), row_tile)
         gate_val, up_val, sig = activations(gate_v, up_v, rows)
         hidden_t[:, rows] = jnp.transpose(gate_val * sig * up_val).astype(jnp.bfloat16)
+
+    def hidden_part(part):
+        gate_load(part).wait()
+        up_load(part).wait()
+        for k in range(2):
+            make_hidden(2 * part + k)
 
     def finish_rows(tile):
         rows = pl.ds(pl.multiple_of(tile * row_tile, row_tile), row_tile)
@@ -161,6 +167,14 @@
         slope = sig * (1.0 + gate_val * (1.0 - sig))
         gate_v[rows, :] = (grad * up_val * slope).astype(jnp.bfloat16)
 
+    def stage_zero(u):
+        def act(p, n):
+            for target in (across_id, far_id, up_id, down_id):
+                push(u, p, n, shard, target, 0)
+            push(u, p, n, shard, sibling_id, 2)
+
+        per_unit(u, act)
+
     def during(t, delay, body):
         @pl.when(jnp.logical_and(t >= delay, t < n_units + delay))
         def _():
@@ -169,7 +183,7 @@
     def step(t, carry):
         def weight_grad(u):
             def act(p, n):
-                arrived(u, n, 3, 8)
+                arrived(u, n, 2, 8)
                 grad = jnp.dot(hidden_t[...], rows_of(p, n), preferred_element_type=jnp.float32)
                 total[:, columns(p, n)] = grad
                 for k in range(n):
@@ -178,38 +192,22 @@
 
             per_unit(u, act)
 
-        def stage_three(u):
-            def act(p, n):
-                arrived(u, n, 2, 1)
-                push(u, p, n, at(z_other, 2), sibling_id, 3)
-
-            per_unit(u, act)
-
         def stage_two(u):
             def act(p, n):
                 arrived(u, n, 1, 3)
-                push(u, p, n, far_id, across_id, 2)
-                for b in (far_id, at(z_other, 1), at(z_other, -1)):
-                    push(u, p, n, b, sibling_id, 3)
+                for step_y in (1, -1, 2):
+                    push(u, p, n, at(z_other, step_y), sibling_id, 2)
 
             per_unit(u, act)
 
         def stage_one(u):
             def act(p, n):
-                arrived(u, n, 0, 3)
+                arrived(u, n, 0, 4)
+                push(u, p, n, far_id, across_id, 1)
                 push(u, p, n, across_id, up_id, 1)
                 push(u, p, n, across_id, down_id, 1)
-                push(u, p, n, at(z_base, -way), at(z_base, way), 1)
-                for b in (across_id, up_id, down_id):
-                    push(u, p, n, b, sibling_id, 3)
-
-            per_unit(u, act)
-
-        def stage_zero(u):
-            def act(p, n):
-                for target in (across_id, up_id, down_id):
-                    push(u, p, n, shard, target, 0)
-                push(u, p, n, shard, sibling_id, 3)
+                for b in (across_id, up_id, down_id, far_id):
+                    push(u, p, n, b, sibling_id, 2)
 
             per_unit(u, act)
 
@@ -245,46 +243,49 @@
 
             per_unit(u, act)
 
-        during(t, 4, weight_grad)
-        during(t, 3, stage_three)
+        @pl.when(t < n_units - 1)
+        def _():
+            stage_zero(t + 1)
+
+        during(t, 3, weight_grad)
+        during(t, 1, stage_one)
         during(t, 2, stage_two)
-        during(t, 1, stage_one)
-        during(t, 0, stage_zero)
-
-        @pl.when(t < 4)
-        def _():
-            gate_load(t).wait()
-            up_load(t).wait()
-            for k in range(2):
-                make_hidden(2 * t + k)
-
-        @pl.when(t == 1)
-        def _():
+
+        @pl.when(t == 0)
+        def _():
+            for part in range(2):
+                hidden_part(part)
             rest_load.wait()
 
             @pl.loop(2, n_pieces)
             def _(p):
                 mask_piece(p)
 
-        @pl.when(t == 4)
+            squares[...] = jnp.zeros_like(squares)
+
+        @pl.when(jnp.logical_and(t >= 1, t < 3))
+        def _():
+            hidden_part(t + 1)
+
+        @pl.when(t == 3)
         def _():
             master_load.wait()
             d_hidden[...] = jnp.zeros_like(d_hidden)
-            squares[...] = jnp.zeros_like(squares)
-
-        during(t, 4, data_grad)
-        during(t, 5, pair_sum)
-
-        @pl.when(jnp.logical_and(t >= n_units + 3, t < n_units + 5))
+
+        during(t, 3, data_grad)
+        during(t, 4, pair_sum)
+
+        @pl.when(jnp.logical_and(t >= n_units + 2, t < n_units + 4))
         def _():
             @pl.loop(0, n_tiles // 2)
             def _(k):
-                finish_rows((t - n_units - 3) * (n_tiles // 2) + k)
-
-        during(t, 7, quad_sum)
+                finish_rows((t - n_units - 2) * (n_tiles // 2) + k)
+
+        during(t, 6, quad_sum)
         return carry
 
-    lax.fori_loop(0, n_units + 7, step, 0)
+    stage_zero(jnp.int32(0))
+    lax.fori_loop(0, n_units + 6, step, 0)
 
     @pl.loop(0, n_units)
     def _(u):
@@ -367,7 +368,7 @@
             pltpu.VMEM(pieces, jnp.bfloat16),
             dma((11,)),
             dma((n_units,)),
-            dma((n_units, 4)),
+            dma((n_units, 3)),
             dma((n_pieces,)),
             dma((n_pieces,)),
             dma((n_pieces,)),

time: 116 us -> 104 us (0.90)
  Pallas kernels: 115 us -> 103 us
    pallas_call x1, Pallas kernels: 110 us -> 98.7 us  [per_device(): pl.pallas_call(kernel, out_shape=(pltpu.VMEM((n_rows, n_hidden), jnp.bflo...]
where the time goes in v4:
time: 104 us
  Pallas kernels  103 us (99%)
  between operations  1.29 us (1%)
    pallas_call x1, Pallas kernels, per_device(): pl.pallas_call(kernel, out_shape=(pltpu.VMEM((n_rows, n_hidden), jnp.bflo...  98.7 us
    pallas_call x1, Pallas kernels, per_device(): pl.pallas_call(finish, out_shape=(jax.ShapeDtypeStruct((n_rows, n_hidden)...  4.13 us

profile of v4, /device:TPU:0, one launch (start us, length us, event | category | flops | bytes accessed | tf_op | source)
XLA Modules:
  0.0 104.2 jit_solution(7369089876463726433)
XLA Ops:
  1.3 98.7 %shard_map.85 = (bf16[2048,512]{1,0:T(8,128)(2,1)S(1)}, bf16[2048,512]{1,0:T(8,128)(2,1)S(1)}, f32[512,3072]{1,0:T(8,128)S(1)}, f32[512,3072]{1,0:T(8,128)S(1)}, f32[512,128]{1,0:T(8,128)S(1)}) custom-call(bf16[128,3072]{1,0:T(8,128)(2,1)} %bitcast.10, bf16[2048,512]{1,0:T(8,128)(2,1)} %bitcast.8, bf16[2048,512]{1,0:T(8,128)(2,1)} %bitcast.9, ...), custom_call_target="tpu_custom_call" | custom-call | tf_op jit(solution)/shard_map/pallas_call | solution.py:348
  100.0 4.1 %shard_map.86 = (bf16[2048,512]{1,0:T(8,128)(2,1)}, bf16[2048,512]{1,0:T(8,128)(2,1)}, f32[512,3072]{1,0:T(8,128)}) custom-call(bf16[2048,512]{1,0:T(8,128)(2,1)S(1)} %get-tuple-element.11.gate_v, bf16[2048,512]{1,0:T(8,128)(2,1)S(1)} %get-tuple-element.12.up_v, f32[512,3072]{1,0:T(8,128)S(1)} %get-tuple-element.13.master_v, ...), custom_call_target="tpu_custom_call" | custom-call | tf_op jit(solution)/shard_map/pallas_call | solution.py:381

commit v5 on v4

--- a/solution.py
+++ b/solution.py
@@ -52,6 +52,7 @@
     barrier = pltpu.get_barrier_semaphore()
     for peer in (
         (expert, up_id), (expert, down_id), (expert, far_id), (expert, across_id),
+        (expert, at(z_other, 1)), (expert, at(z_other, -1)), (expert, at(z_other, 2)),
         (expert, sibling_id), (pair_id, shard), (quad_id, shard),
     ):
         pl.semaphore_signal(barrier, inc=1, device_id=peer, device_id_type=MESH)
@@ -112,21 +113,39 @@
         blocks = some_blocks(n, k)
         pltpu.make_async_copy(blocks, blocks, gather_recv.at[u, stage]).wait()
 
-    def exchange(out, landing, send_sem, recv_sem, target, p):
+    quarter_rows = n_hidden // 4
+
+    def part_rows(q):
+        return pl.ds(0, n_hidden) if q is None else pl.ds(q * quarter_rows, quarter_rows)
+
+    def exchange(out, landing, send_sem, recv_sem, target, p, q):
+        index = p if q is None else p + q
         return pltpu.make_async_remote_copy(
-            src_ref=out.at[p],
-            dst_ref=landing.at[p],
-            send_sem=send_sem.at[p],
-            recv_sem=recv_sem.at[p],
+            src_ref=out.at[p, part_rows(q)],
+            dst_ref=landing.at[p, part_rows(q)],
+            send_sem=send_sem.at[index],
+            recv_sem=recv_sem.at[index],
             device_id=(target, shard),
             device_id_type=MESH,
         )
 
-    def pair_copy(p):
-        return exchange(pair_out, pair_in, pair_send, pair_recv, pair_id, p)
-
-    def quad_copy(p):
-        return exchange(quad_out, quad_in, quad_send, quad_recv, quad_id, p)
+    def pair_copy(p, q):
+        return exchange(pair_out, pair_in, pair_send, pair_recv, pair_id, p, q)
+
+    def quad_copy(p, q):
+        return exchange(quad_out, quad_in, quad_send, quad_recv, quad_id, p, q)
+
+    def per_part(u, p, n, act):
+        act(p, None)
+        if n == 2:
+            @pl.when(u < n_units - 1)
+            def _():
+                act(p + 1, None)
+
+            @pl.when(u == n_units - 1)
+            def _():
+                for q in range(4):
+                    act(n_pieces - 1, q)
 
     def columns(p, n):
         return pl.ds(pl.multiple_of(p * piece, piece), n * piece)
@@ -146,7 +165,7 @@
     first_load.wait()
     mask_piece(0)
     mask_piece(1)
-    pl.semaphore_wait(barrier, 7)
+    pl.semaphore_wait(barrier, 10)
 
     def make_hidden(tile):
         rows = pl.ds(pl.multiple_of(tile * row_tile, row_tile), row_tile)
@@ -169,7 +188,10 @@
 
     def stage_zero(u):
         def act(p, n):
-            for target in (across_id, far_id, up_id, down_id):
+            targets = (across_id, far_id, up_id, down_id)
+            if n == 1:
+                targets = (at(z_other, 2), at(z_other, 1), at(z_other, -1)) + targets
+            for target in targets:
                 push(u, p, n, shard, target, 0)
             push(u, p, n, shard, sibling_id, 2)
 
@@ -188,25 +210,29 @@
                 total[:, columns(p, n)] = grad
                 for k in range(n):
                     pair_out[p + k] = grad[:, k * piece : (k + 1) * piece].astype(jnp.bfloat16)
-                    pair_copy(p + k).start()
-
-            per_unit(u, act)
+                per_part(u, p, n, lambda p, q: pair_copy(p, q).start())
+
+            return act
 
         def stage_two(u):
-            def act(p, n):
-                arrived(u, n, 1, 3)
+            @pl.when(u >= 2)
+            def _():
+                arrived(u, 2, 1, 3)
                 for step_y in (1, -1, 2):
-                    push(u, p, n, at(z_other, step_y), sibling_id, 2)
-
-            per_unit(u, act)
+                    push(u, 2 * u - 2, 2, at(z_other, step_y), sibling_id, 2)
 
         def stage_one(u):
             def act(p, n):
-                arrived(u, n, 0, 4)
-                push(u, p, n, far_id, across_id, 1)
-                push(u, p, n, across_id, up_id, 1)
-                push(u, p, n, across_id, down_id, 1)
-                for b in (across_id, up_id, down_id, far_id):
+                blocks = (across_id, up_id, down_id, far_id)
+                if n == 1:
+                    arrived(u, n, 0, 7)
+                    blocks += (at(z_other, 1), at(z_other, -1), at(z_other, 2))
+                else:
+                    arrived(u, n, 0, 4)
+                    push(u, p, n, far_id, across_id, 1)
+                    push(u, p, n, across_id, up_id, 1)
+                    push(u, p, n, across_id, down_id, 1)
+                for b in blocks:
                     push(u, p, n, b, sibling_id, 2)
 
             per_unit(u, act)
@@ -221,35 +247,42 @@
                 )
 
         def pair_sum(u):
-            def act(p, n):
-                for k in range(n):
-                    pair_copy(p + k).wait_recv()
-                    part = columns(p + k, 1)
-                    both = total[:, part] + same_pair * pair_in[p + k].astype(jnp.float32)
-                    total[:, part] = both
-                    quad_out[p + k] = both.astype(jnp.bfloat16)
-                    quad_copy(p + k).start()
-
-            per_unit(u, act)
+            def one(p, q):
+                pair_copy(p, q).wait_recv()
+                rows, cols = part_rows(q), columns(p, 1)
+                received = pair_in[p, rows, :].astype(jnp.float32)
+                both = total[rows, cols] + same_pair * received
+                total[rows, cols] = both
+                quad_out[p, rows, :] = both.astype(jnp.bfloat16)
+                quad_copy(p, q).start()
+
+            per_unit(u, lambda p, n: per_part(u, p, n, one))
 
         def quad_sum(u):
-            def act(p, n):
-                for k in range(n):
-                    quad_copy(p + k).wait_recv()
-                    part = columns(p + k, 1)
-                    whole = total[:, part] + same_quad * quad_in[p + k].astype(jnp.float32)
-                    total[:, part] = whole
-                    squares[...] += whole * whole
-
-            per_unit(u, act)
-
-        @pl.when(t < n_units - 1)
-        def _():
-            stage_zero(t + 1)
-
-        during(t, 3, weight_grad)
+            def one(p, q):
+                quad_copy(p, q).wait_recv()
+                rows, cols = part_rows(q), columns(p, 1)
+                received = quad_in[p, rows, :].astype(jnp.float32)
+                whole = total[rows, cols] + same_quad * received
+                total[rows, cols] = whole
+                squares[rows, :] += whole * whole
+
+            per_unit(u, lambda p, n: per_part(u, p, n, one))
+
+        @pl.when(jnp.logical_and(t >= 2, t < 4))
+        def _():
+            weight_grad(t - 2)(t - 2, 1)
+
+        @pl.when(jnp.logical_and(t >= 5, t < n_units + 3))
+        def _():
+            weight_grad(t - 3)(2 * (t - 3) - 2, 2)
+
         during(t, 1, stage_one)
         during(t, 2, stage_two)
+
+        @pl.when(t < n_units - 1)
+        def _():
+            stage_zero(t + 1)
 
         @pl.when(t == 0)
         def _():
@@ -263,9 +296,10 @@
 
             squares[...] = jnp.zeros_like(squares)
 
-        @pl.when(jnp.logical_and(t >= 1, t < 3))
-        def _():
-            hidden_part(t + 1)
+        @pl.when(t == 1)
+        def _():
+            for part in range(2, 4):
+                hidden_part(part)
 
         @pl.when(t == 3)
         def _():
@@ -292,9 +326,12 @@
         def act(p, n):
             blocks = some_blocks(n, 15)
             pltpu.make_async_copy(blocks, blocks, gather_send.at[u]).wait()
-            for k in range(n):
-                pair_copy(p + k).wait_send()
-                quad_copy(p + k).wait_send()
+
+            def sent(p, q):
+                pair_copy(p, q).wait_send()
+                quad_copy(p, q).wait_send()
+
+            per_part(u, p, n, sent)
 
         per_unit(u, act)
 
@@ -369,10 +406,10 @@
             dma((11,)),
             dma((n_units,)),
             dma((n_units, 3)),
-            dma((n_pieces,)),
-            dma((n_pieces,)),
-            dma((n_pieces,)),
-            dma((n_pieces,)),
+            dma((n_pieces + 3,)),
+            dma((n_pieces + 3,)),
+            dma((n_pieces + 3,)),
+            dma((n_pieces + 3,)),
         ],
         compiler_params=pltpu.CompilerParams(
             collective_id=0, has_side_effects=True, vmem_limit_bytes=40 * 2**20

time: 104 us -> 106 us (1.019)
    pallas_call x1, Pallas kernels: 98.7 us -> 100 us  [per_device(): pl.pallas_call(kernel, out_shape=(pltpu.VMEM((n_rows, n_hidden), jnp.bflo...]
where the time goes in v5:
time: 106 us
  Pallas kernels  104 us (98%)
  between operations  1.29 us (1%)
    pallas_call x1, Pallas kernels, per_device(): pl.pallas_call(kernel, out_shape=(pltpu.VMEM((n_rows, n_hidden), jnp.bflo...  100 us
    pallas_call x1, Pallas kernels, per_device(): pl.pallas_call(finish, out_shape=(jax.ShapeDtypeStruct((n_rows, n_hidden)...  4.13 us

profile of v5, /device:TPU:0, one launch (start us, length us, event | category | flops | bytes accessed | tf_op | source)
XLA Modules:
  0.0 105.7 jit_solution(9452761539441258210)
XLA Ops:
  1.3 100.3 %shard_map.85 = (bf16[2048,512]{1,0:T(8,128)(2,1)S(1)}, bf16[2048,512]{1,0:T(8,128)(2,1)S(1)}, f32[512,3072]{1,0:T(8,128)S(1)}, f32[512,3072]{1,0:T(8,128)S(1)}, f32[512,128]{1,0:T(8,128)S(1)}) custom-call(bf16[128,3072]{1,0:T(8,128)(2,1)} %bitcast.10, bf16[2048,512]{1,0:T(8,128)(2,1)} %bitcast.8, bf16[2048,512]{1,0:T(8,128)(2,1)} %bitcast.9, ...), custom_call_target="tpu_custom_call" | custom-call | tf_op jit(solution)/shard_map/pallas_call | solution.py:385
  101.6 4.1 %shard_map.86 = (bf16[2048,512]{1,0:T(8,128)(2,1)}, bf16[2048,512]{1,0:T(8,128)(2,1)}, f32[512,3072]{1,0:T(8,128)}) custom-call(bf16[2048,512]{1,0:T(8,128)(2,1)S(1)} %get-tuple-element.11.gate_v, bf16[2048,512]{1,0:T(8,128)(2,1)S(1)} %get-tuple-element.12.up_v, f32[512,3072]{1,0:T(8,128)S(1)} %get-tuple-element.13.master_v, ...), custom_call_target="tpu_custom_call" | custom-call | tf_op jit(solution)/shard_map/pallas_call | solution.py:418

commit v6 on v5

--- a/solution.py
+++ b/solution.py
@@ -24,8 +24,8 @@
     grad_hbm, gate_hbm, up_hbm, counts_ref, place_ref, master_hbm,
     gate_v, up_v, master_v, total, squares,
     grad_v, rows_v, hidden_t, d_hidden, weight_t,
-    pair_out, pair_in, quad_out, quad_in,
-    load_sem, gather_send, gather_recv, pair_send, pair_recv, quad_send, quad_recv,
+    first_out, first_in, second_out, second_in,
+    load_sem, gather_send, gather_recv, first_send, first_recv, second_send, second_recv,
 ):
     expert, shard = lax.axis_index("expert"), lax.axis_index("shard")
     block, width = grad_v.shape
@@ -52,7 +52,6 @@
     barrier = pltpu.get_barrier_semaphore()
     for peer in (
         (expert, up_id), (expert, down_id), (expert, far_id), (expert, across_id),
-        (expert, at(z_other, 1)), (expert, at(z_other, -1)), (expert, at(z_other, 2)),
         (expert, sibling_id), (pair_id, shard), (quad_id, shard),
     ):
         pl.semaphore_signal(barrier, inc=1, device_id=peer, device_id_type=MESH)
@@ -118,33 +117,41 @@
     def part_rows(q):
         return pl.ds(0, n_hidden) if q is None else pl.ds(q * quarter_rows, quarter_rows)
 
-    def exchange(out, landing, send_sem, recv_sem, target, p, q):
-        index = p if q is None else p + q
+    def exchange(out, landing, send_sem, recv_sem, swap, p, q):
+        index = p if q is None else n_pieces - 2 + 4 * (p - n_pieces + 2) + q
+        odd = (p + swap) % 2
         return pltpu.make_async_remote_copy(
             src_ref=out.at[p, part_rows(q)],
             dst_ref=landing.at[p, part_rows(q)],
             send_sem=send_sem.at[index],
             recv_sem=recv_sem.at[index],
-            device_id=(target, shard),
+            device_id=(pair_id * (1 - odd) + quad_id * odd, shard),
             device_id_type=MESH,
         )
 
-    def pair_copy(p, q):
-        return exchange(pair_out, pair_in, pair_send, pair_recv, pair_id, p, q)
-
-    def quad_copy(p, q):
-        return exchange(quad_out, quad_in, quad_send, quad_recv, quad_id, p, q)
+    def first_copy(p, q):
+        return exchange(first_out, first_in, first_send, first_recv, 0, p, q)
+
+    def second_copy(p, q):
+        return exchange(second_out, second_in, second_send, second_recv, 1, p, q)
+
+    def same_expert(p, swap):
+        odd = jnp.asarray((p + swap) % 2, jnp.float32)
+        return same_pair * (1.0 - odd) + same_quad * odd
 
     def per_part(u, p, n, act):
-        act(p, None)
-        if n == 2:
+        if n == 1:
+            act(p, None)
+        else:
             @pl.when(u < n_units - 1)
             def _():
+                act(p, None)
                 act(p + 1, None)
 
             @pl.when(u == n_units - 1)
             def _():
                 for q in range(4):
+                    act(n_pieces - 2, q)
                     act(n_pieces - 1, q)
 
     def columns(p, n):
@@ -165,7 +172,7 @@
     first_load.wait()
     mask_piece(0)
     mask_piece(1)
-    pl.semaphore_wait(barrier, 10)
+    pl.semaphore_wait(barrier, 7)
 
     def make_hidden(tile):
         rows = pl.ds(pl.multiple_of(tile * row_tile, row_tile), row_tile)
@@ -188,10 +195,7 @@
 
     def stage_zero(u):
         def act(p, n):
-            targets = (across_id, far_id, up_id, down_id)
-            if n == 1:
-                targets = (at(z_other, 2), at(z_other, 1), at(z_other, -1)) + targets
-            for target in targets:
+            for target in (across_id, far_id, up_id, down_id):
                 push(u, p, n, shard, target, 0)
             push(u, p, n, shard, sibling_id, 2)
 
@@ -209,30 +213,26 @@
                 grad = jnp.dot(hidden_t[...], rows_of(p, n), preferred_element_type=jnp.float32)
                 total[:, columns(p, n)] = grad
                 for k in range(n):
-                    pair_out[p + k] = grad[:, k * piece : (k + 1) * piece].astype(jnp.bfloat16)
-                per_part(u, p, n, lambda p, q: pair_copy(p, q).start())
-
-            return act
+                    first_out[p + k] = grad[:, k * piece : (k + 1) * piece].astype(jnp.bfloat16)
+                per_part(u, p, n, lambda p, q: first_copy(p, q).start())
+
+            per_unit(u, act)
 
         def stage_two(u):
-            @pl.when(u >= 2)
-            def _():
-                arrived(u, 2, 1, 3)
+            def act(p, n):
+                arrived(u, n, 1, 3)
                 for step_y in (1, -1, 2):
-                    push(u, 2 * u - 2, 2, at(z_other, step_y), sibling_id, 2)
+                    push(u, p, n, at(z_other, step_y), sibling_id, 2)
+
+            per_unit(u, act)
 
         def stage_one(u):
             def act(p, n):
-                blocks = (across_id, up_id, down_id, far_id)
-                if n == 1:
-                    arrived(u, n, 0, 7)
-                    blocks += (at(z_other, 1), at(z_other, -1), at(z_other, 2))
-                else:
-                    arrived(u, n, 0, 4)
-                    push(u, p, n, far_id, across_id, 1)
-                    push(u, p, n, across_id, up_id, 1)
-                    push(u, p, n, across_id, down_id, 1)
-                for b in blocks:
+                arrived(u, n, 0, 4)
+                push(u, p, n, far_id, across_id, 1)
+                push(u, p, n, across_id, up_id, 1)
+                push(u, p, n, across_id, down_id, 1)
+                for b in (across_id, up_id, down_id, far_id):
                     push(u, p, n, b, sibling_id, 2)
 
             per_unit(u, act)
@@ -246,37 +246,30 @@
                     rows_of(p, 2), weight_t[...], preferred_element_type=jnp.float32
                 )
 
-        def pair_sum(u):
+        def first_sum(u):
             def one(p, q):
-                pair_copy(p, q).wait_recv()
+                first_copy(p, q).wait_recv()
                 rows, cols = part_rows(q), columns(p, 1)
-                received = pair_in[p, rows, :].astype(jnp.float32)
-                both = total[rows, cols] + same_pair * received
+                received = first_in[p, rows, :].astype(jnp.float32)
+                both = total[rows, cols] + same_expert(p, 0) * received
                 total[rows, cols] = both
-                quad_out[p, rows, :] = both.astype(jnp.bfloat16)
-                quad_copy(p, q).start()
+                second_out[p, rows, :] = both.astype(jnp.bfloat16)
+                second_copy(p, q).start()
 
             per_unit(u, lambda p, n: per_part(u, p, n, one))
 
-        def quad_sum(u):
+        def second_sum(u):
             def one(p, q):
-                quad_copy(p, q).wait_recv()
+                second_copy(p, q).wait_recv()
                 rows, cols = part_rows(q), columns(p, 1)
-                received = quad_in[p, rows, :].astype(jnp.float32)
-                whole = total[rows, cols] + same_quad * received
+                received = second_in[p, rows, :].astype(jnp.float32)
+                whole = total[rows, cols] + same_expert(p, 1) * received
                 total[rows, cols] = whole
                 squares[rows, :] += whole * whole
 
             per_unit(u, lambda p, n: per_part(u, p, n, one))
 
-        @pl.when(jnp.logical_and(t >= 2, t < 4))
-        def _():
-            weight_grad(t - 2)(t - 2, 1)
-
-        @pl.when(jnp.logical_and(t >= 5, t < n_units + 3))
-        def _():
-            weight_grad(t - 3)(2 * (t - 3) - 2, 2)
-
+        during(t, 3, weight_grad)
         during(t, 1, stage_one)
         during(t, 2, stage_two)
 
@@ -307,7 +300,7 @@
             d_hidden[...] = jnp.zeros_like(d_hidden)
 
         during(t, 3, data_grad)
-        during(t, 4, pair_sum)
+        during(t, 4, first_sum)
 
         @pl.when(jnp.logical_and(t >= n_units + 2, t < n_units + 4))
         def _():
@@ -315,7 +308,7 @@
             def _(k):
                 finish_rows((t - n_units - 2) * (n_tiles // 2) + k)
 
-        during(t, 6, quad_sum)
+        during(t, 6, second_sum)
         return carry
 
     stage_zero(jnp.int32(0))
@@ -328,8 +321,8 @@
             pltpu.make_async_copy(blocks, blocks, gather_send.at[u]).wait()
 
             def sent(p, q):
-                pair_copy(p, q).wait_send()
-                quad_copy(p, q).wait_send()
+                first_copy(p, q).wait_send()
+                second_copy(p, q).wait_send()
 
             per_part(u, p, n, sent)
 
@@ -406,10 +399,10 @@
             dma((11,)),
             dma((n_units,)),
             dma((n_units, 3)),
-            dma((n_pieces + 3,)),
-            dma((n_pieces + 3,)),
-            dma((n_pieces + 3,)),
-            dma((n_pieces + 3,)),
+            dma((n_pieces + 6,)),
+            dma((n_pieces + 6,)),
+            dma((n_pieces + 6,)),
+            dma((n_pieces + 6,)),
         ],
         compiler_params=pltpu.CompilerParams(
             collective_id=0, has_side_effects=True, vmem_limit_bytes=40 * 2**20

time: 106 us -> 99.5 us (0.939)
  Pallas kernels: 104 us -> 97.8 us
    pallas_call x1, Pallas kernels: 100 us -> 93.7 us  [per_device(): pl.pallas_call(kernel, out_shape=(pltpu.VMEM((n_rows, n_hidden), jnp.bflo...]
where the time goes in v6:
time: 99.5 us; the launch traced here: 99.1 us
  Pallas kernels  97.8 us (98%)
  between operations  1.29 us (1%)
    pallas_call x1, Pallas kernels, per_device(): pl.pallas_call(kernel, out_shape=(pltpu.VMEM((n_rows, n_hidden), jnp.bflo...  93.7 us
    pallas_call x1, Pallas kernels, per_device(): pl.pallas_call(finish, out_shape=(jax.ShapeDtypeStruct((n_rows, n_hidden)...  4.13 us

profile of v6, /device:TPU:0, one launch (start us, length us, event | category | flops | bytes accessed | tf_op | source)
XLA Modules:
  0.0 99.1 jit_solution(15900230671260771437)
XLA Ops:
  1.3 93.7 %shard_map.85 = (bf16[2048,512]{1,0:T(8,128)(2,1)S(1)}, bf16[2048,512]{1,0:T(8,128)(2,1)S(1)}, f32[512,3072]{1,0:T(8,128)S(1)}, f32[512,3072]{1,0:T(8,128)S(1)}, f32[512,128]{1,0:T(8,128)S(1)}) custom-call(bf16[128,3072]{1,0:T(8,128)(2,1)} %bitcast.10, bf16[2048,512]{1,0:T(8,128)(2,1)} %bitcast.8, bf16[2048,512]{1,0:T(8,128)(2,1)} %bitcast.9, ...), custom_call_target="tpu_custom_call" | custom-call | tf_op jit(solution)/shard_map/pallas_call | solution.py:378
  95.0 4.1 %shard_map.86 = (bf16[2048,512]{1,0:T(8,128)(2,1)}, bf16[2048,512]{1,0:T(8,128)(2,1)}, f32[512,3072]{1,0:T(8,128)}) custom-call(bf16[2048,512]{1,0:T(8,128)(2,1)S(1)} %get-tuple-element.11.gate_v, bf16[2048,512]{1,0:T(8,128)(2,1)S(1)} %get-tuple-element.12.up_v, f32[512,3072]{1,0:T(8,128)S(1)} %get-tuple-element.13.master_v, ...), custom_call_target="tpu_custom_call" | custom-call | tf_op jit(solution)/shard_map/pallas_call | solution.py:411

commit v7 on v6

--- a/solution.py
+++ b/solution.py
@@ -30,7 +30,7 @@
     expert, shard = lax.axis_index("expert"), lax.axis_index("shard")
     block, width = grad_v.shape
     n_pieces = width // piece
-    n_units = n_pieces // 2 + 1
+    n_units = n_pieces // 2
     n_rows, n_hidden = gate_v.shape
     n_tiles = n_rows // row_tile
 
@@ -90,13 +90,7 @@
         return rows_v.at[pl.ds(0, n), pl.ds(0, k * block)]
 
     def per_unit(u, act):
-        @pl.when(u < 2)
-        def _():
-            act(u, 1)
-
-        @pl.when(u >= 2)
-        def _():
-            act(2 * u - 2, 2)
+        act(2 * u, 2)
 
     def push(u, p, n, b, target, stage):
         pltpu.make_async_remote_copy(
@@ -238,13 +232,13 @@
             per_unit(u, act)
 
         def data_grad(u):
-            @pl.when(u >= 1)
-            def _():
-                p = 2 * u - 2
+            def add(p):
                 weight_t[...] = jnp.transpose(master_v[:, columns(p, 2)]).astype(jnp.bfloat16)
                 d_hidden[...] += jnp.dot(
                     rows_of(p, 2), weight_t[...], preferred_element_type=jnp.float32
                 )
+
+            add(2 * u)
 
         def first_sum(u):
             def one(p, q):
@@ -266,21 +260,23 @@
                 whole = total[rows, cols] + same_expert(p, 1) * received
                 total[rows, cols] = whole
                 squares[rows, :] += whole * whole
-
-            per_unit(u, lambda p, n: per_part(u, p, n, one))
+                first_copy(p, q).wait_send()
+                second_copy(p, q).wait_send()
+
+            def act(p, n):
+                blocks = some_blocks(n, 15)
+                pltpu.make_async_copy(blocks, blocks, gather_send.at[u]).wait()
+                per_part(u, p, n, one)
+
+            per_unit(u, act)
 
         during(t, 3, weight_grad)
         during(t, 1, stage_one)
         during(t, 2, stage_two)
 
-        @pl.when(t < n_units - 1)
-        def _():
-            stage_zero(t + 1)
-
         @pl.when(t == 0)
         def _():
-            for part in range(2):
-                hidden_part(part)
+            hidden_part(0)
             rest_load.wait()
 
             @pl.loop(2, n_pieces)
@@ -289,7 +285,15 @@
 
             squares[...] = jnp.zeros_like(squares)
 
+        @pl.when(t < n_units - 1)
+        def _():
+            stage_zero(t + 1)
+
         @pl.when(t == 1)
+        def _():
+            hidden_part(1)
+
+        @pl.when(t == 2)
         def _():
             for part in range(2, 4):
                 hidden_part(part)
@@ -313,20 +317,6 @@
 
     stage_zero(jnp.int32(0))
     lax.fori_loop(0, n_units + 6, step, 0)
-
-    @pl.loop(0, n_units)
-    def _(u):
-        def act(p, n):
-            blocks = some_blocks(n, 15)
-            pltpu.make_async_copy(blocks, blocks, gather_send.at[u]).wait()
-
-            def sent(p, q):
-                first_copy(p, q).wait_send()
-                second_copy(p, q).wait_send()
-
-            per_part(u, p, n, sent)
-
-        per_unit(u, act)
 
 
 def finish(
@@ -369,7 +359,7 @@
     block, width = grad_out.shape[1:]
     n_rows, n_hidden = gate_pre.shape[1:]
     n_pieces = width // piece
-    n_units = n_pieces // 2 + 1
+    n_units = n_pieces // 2
     hbm = pl.BlockSpec(memory_space=pl.ANY)
     smem = pl.BlockSpec(memory_space=pltpu.SMEM)
     vmem = pl.BlockSpec(memory_space=pltpu.VMEM)

time: 99.5 us -> 98.5 us (0.990)
  Pallas kernels: 97.8 us -> 96.8 us
where the time goes in v7:
time: 98.5 us; the launch traced here: 98.1 us
  Pallas kernels  96.8 us (98%)
  between operations  1.29 us (1%)
    pallas_call x1, Pallas kernels, per_device(): pl.pallas_call(kernel, out_shape=(pltpu.VMEM((n_rows, n_hidden), jnp.bflo...  92.7 us
    pallas_call x1, Pallas kernels, per_device(): pl.pallas_call(finish, out_shape=(jax.ShapeDtypeStruct((n_rows, n_hidden)...  4.13 us

profile of v7, /device:TPU:0, one launch (start us, length us, event | category | flops | bytes accessed | tf_op | source)
XLA Modules:
  0.0 98.1 jit_solution(16847630289499544401)
XLA Ops:
  1.3 92.7 %shard_map.85 = (bf16[2048,512]{1,0:T(8,128)(2,1)S(1)}, bf16[2048,512]{1,0:T(8,128)(2,1)S(1)}, f32[512,3072]{1,0:T(8,128)S(1)}, f32[512,3072]{1,0:T(8,128)S(1)}, f32[512,128]{1,0:T(8,128)S(1)}) custom-call(bf16[128,3072]{1,0:T(8,128)(2,1)} %bitcast.10, bf16[2048,512]{1,0:T(8,128)(2,1)} %bitcast.8, bf16[2048,512]{1,0:T(8,128)(2,1)} %bitcast.9, ...), custom_call_target="tpu_custom_call" | custom-call | tf_op jit(solution)/shard_map/pallas_call | solution.py:368
  94.0 4.1 %shard_map.86 = (bf16[2048,512]{1,0:T(8,128)(2,1)}, bf16[2048,512]{1,0:T(8,128)(2,1)}, f32[512,3072]{1,0:T(8,128)}) custom-call(bf16[2048,512]{1,0:T(8,128)(2,1)S(1)} %get-tuple-element.11.gate_v, bf16[2048,512]{1,0:T(8,128)(2,1)S(1)} %get-tuple-element.12.up_v, f32[512,3072]{1,0:T(8,128)S(1)} %get-tuple-element.13.master_v, ...), custom_call_target="tpu_custom_call" | custom-call | tf_op jit(solution)/shard_map/pallas_call | solution.py:401

commit v8 on v7

--- a/solution.py
+++ b/solution.py
@@ -49,6 +49,26 @@
     pair_id = expert + 1 - 2 * (expert % 2)
     quad_id = expert + 3 - 2 * (expert % 4)
 
+    def load(src, dst, index):
+        return pltpu.make_async_copy(src, dst, load_sem.at[index])
+
+    quarter = n_rows // 4
+
+    def gate_load(part):
+        rows = pl.ds(pl.multiple_of(part * quarter, quarter), quarter)
+        return load(gate_hbm.at[rows], gate_v.at[rows], 3 + part)
+
+    def up_load(part):
+        rows = pl.ds(pl.multiple_of(part * quarter, quarter), quarter)
+        return load(up_hbm.at[rows], up_v.at[rows], 7 + part)
+
+    first, rest = pl.ds(0, chunk), pl.ds(chunk, width - chunk)
+    first_load = load(grad_hbm.at[:, first], grad_v.at[:, first], 0)
+    rest_load = load(grad_hbm.at[:, rest], grad_v.at[:, rest], 1)
+    master_load = load(master_hbm, master_v, 2)
+    first_load.start()
+    rest_load.start()
+
     barrier = pltpu.get_barrier_semaphore()
     for peer in (
         (expert, up_id), (expert, down_id), (expert, far_id), (expert, across_id),
@@ -56,28 +76,9 @@
     ):
         pl.semaphore_signal(barrier, inc=1, device_id=peer, device_id_type=MESH)
 
-    def load(src, dst, index):
-        return pltpu.make_async_copy(src, dst, load_sem.at[index])
-
-    quarter = n_rows // 4
-
-    def gate_load(part):
-        rows = pl.ds(pl.multiple_of(part * quarter, quarter), quarter)
-        return load(gate_hbm.at[rows], gate_v.at[rows], 3 + part)
-
-    def up_load(part):
-        rows = pl.ds(pl.multiple_of(part * quarter, quarter), quarter)
-        return load(up_hbm.at[rows], up_v.at[rows], 7 + part)
-
-    first, rest = pl.ds(0, chunk), pl.ds(chunk, width - chunk)
-    first_load = load(grad_hbm.at[:, first], grad_v.at[:, first], 0)
-    rest_load = load(grad_hbm.at[:, rest], grad_v.at[:, rest], 1)
-    master_load = load(master_hbm, master_v, 2)
-    first_load.start()
     for part in range(4):
         gate_load(part).start()
         up_load(part).start()
-    rest_load.start()
     master_load.start()
 
     same_pair = jnp.where(place_ref[expert] == place_ref[pair_id], 1.0, 0.0)
@@ -276,10 +277,14 @@
 
         @pl.when(t == 0)
         def _():
-            hidden_part(0)
             rest_load.wait()
 
-            @pl.loop(2, n_pieces)
+            mask_piece(2)
+            mask_piece(3)
+
+        @pl.when(t == 1)
+        def _():
+            @pl.loop(4, n_pieces)
             def _(p):
                 mask_piece(p)
 
@@ -289,9 +294,9 @@
         def _():
             stage_zero(t + 1)
 
-        @pl.when(t == 1)
-        def _():
-            hidden_part(1)
+        @pl.when(t < 2)
+        def _():
+            hidden_part(t)
 
         @pl.when(t == 2)
         def _():

time: 98.5 us -> 98.5 us (level)
  no operation moved by 1% of the time
where the time goes in v8:
time: 98.5 us; the launch traced here: 98.1 us
  Pallas kernels  96.8 us (98%)
  between operations  1.29 us (1%)
    pallas_call x1, Pallas kernels, per_device(): pl.pallas_call(kernel, out_shape=(pltpu.VMEM((n_rows, n_hidden), jnp.bflo...  92.7 us
    pallas_call x1, Pallas kernels, per_device(): pl.pallas_call(finish, out_shape=(jax.ShapeDtypeStruct((n_rows, n_hidden)...  4.13 us

profile of v8, /device:TPU:0, one launch (start us, length us, event | category | flops | bytes accessed | tf_op | source)
XLA Modules:
  0.0 98.1 jit_solution(1279311571248892577)
XLA Ops:
  1.3 92.7 %shard_map.85 = (bf16[2048,512]{1,0:T(8,128)(2,1)S(1)}, bf16[2048,512]{1,0:T(8,128)(2,1)S(1)}, f32[512,3072]{1,0:T(8,128)S(1)}, f32[512,3072]{1,0:T(8,128)S(1)}, f32[512,128]{1,0:T(8,128)S(1)}) custom-call(bf16[128,3072]{1,0:T(8,128)(2,1)} %bitcast.10, bf16[2048,512]{1,0:T(8,128)(2,1)} %bitcast.8, bf16[2048,512]{1,0:T(8,128)(2,1)} %bitcast.9, ...), custom_call_target="tpu_custom_call" | custom-call | tf_op jit(solution)/shard_map/pallas_call | solution.py:373
  94.0 4.1 %shard_map.86 = (bf16[2048,512]{1,0:T(8,128)(2,1)}, bf16[2048,512]{1,0:T(8,128)(2,1)}, f32[512,3072]{1,0:T(8,128)}) custom-call(bf16[2048,512]{1,0:T(8,128)(2,1)S(1)} %get-tuple-element.11.gate_v, bf16[2048,512]{1,0:T(8,128)(2,1)S(1)} %get-tuple-element.12.up_v, f32[512,3072]{1,0:T(8,128)S(1)} %get-tuple-element.13.master_v, ...), custom_call_target="tpu_custom_call" | custom-call | tf_op jit(solution)/shard_map/pallas_call | solution.py:406

commit v9 on v8

--- a/solution.py
+++ b/solution.py
@@ -10,7 +10,8 @@
 piece = 128
 chunk = 256
 row_tile = 256
-out_tile = 64
+out_tile = 128
+last_parts = 8
 MESH = pl.DeviceIdType.MESH
 
 
@@ -107,13 +108,13 @@
         blocks = some_blocks(n, k)
         pltpu.make_async_copy(blocks, blocks, gather_recv.at[u, stage]).wait()
 
-    quarter_rows = n_hidden // 4
+    quarter_rows = n_hidden // last_parts
 
     def part_rows(q):
         return pl.ds(0, n_hidden) if q is None else pl.ds(q * quarter_rows, quarter_rows)
 
     def exchange(out, landing, send_sem, recv_sem, swap, p, q):
-        index = p if q is None else n_pieces - 2 + 4 * (p - n_pieces + 2) + q
+        index = p if q is None else n_pieces - 2 + last_parts * (p - n_pieces + 2) + q
         odd = (p + swap) % 2
         return pltpu.make_async_remote_copy(
             src_ref=out.at[p, part_rows(q)],
@@ -145,7 +146,7 @@
 
             @pl.when(u == n_units - 1)
             def _():
-                for q in range(4):
+                for q in range(last_parts):
                     act(n_pieces - 2, q)
                     act(n_pieces - 1, q)
 
@@ -394,10 +395,10 @@
             dma((11,)),
             dma((n_units,)),
             dma((n_units, 3)),
-            dma((n_pieces + 6,)),
-            dma((n_pieces + 6,)),
-            dma((n_pieces + 6,)),
-            dma((n_pieces + 6,)),
+            dma((n_pieces - 2 + 2 * last_parts,)),
+            dma((n_pieces - 2 + 2 * last_parts,)),
+            dma((n_pieces - 2 + 2 * last_parts,)),
+            dma((n_pieces - 2 + 2 * last_parts,)),
         ],
         compiler_params=pltpu.CompilerParams(
             collective_id=0, has_side_effects=True, vmem_limit_bytes=40 * 2**20

time: 98.5 us -> 98.8 us (level)
  no operation moved by 1% of the time
where the time goes in v9:
time: 98.8 us; the launch traced here: 98.4 us
  Pallas kernels  97.1 us (98%)
  between operations  1.29 us (1%)
    pallas_call x1, Pallas kernels, per_device(): pl.pallas_call(kernel, out_shape=(pltpu.VMEM((n_rows, n_hidden), jnp.bflo...  93 us
    pallas_call x1, Pallas kernels, per_device(): pl.pallas_call(finish, out_shape=(jax.ShapeDtypeStruct((n_rows, n_hidden)...  4.16 us

profile of v9, /device:TPU:0, one launch (start us, length us, event | category | flops | bytes accessed | tf_op | source)
XLA Modules:
  0.0 98.4 jit_solution(1168008354012453374)
XLA Ops:
  1.3 93.0 %shard_map.85 = (bf16[2048,512]{1,0:T(8,128)(2,1)S(1)}, bf16[2048,512]{1,0:T(8,128)(2,1)S(1)}, f32[512,3072]{1,0:T(8,128)S(1)}, f32[512,3072]{1,0:T(8,128)S(1)}, f32[512,128]{1,0:T(8,128)S(1)}) custom-call(bf16[128,3072]{1,0:T(8,128)(2,1)} %bitcast.10, bf16[2048,512]{1,0:T(8,128)(2,1)} %bitcast.8, bf16[2048,512]{1,0:T(8,128)(2,1)} %bitcast.9, ...), custom_call_target="tpu_custom_call" | custom-call | tf_op jit(solution)/shard_map/pallas_call | solution.py:374
  94.3 4.2 %shard_map.86 = (bf16[2048,512]{1,0:T(8,128)(2,1)}, bf16[2048,512]{1,0:T(8,128)(2,1)}, f32[512,3072]{1,0:T(8,128)}) custom-call(bf16[2048,512]{1,0:T(8,128)(2,1)S(1)} %get-tuple-element.11.gate_v, bf16[2048,512]{1,0:T(8,128)(2,1)S(1)} %get-tuple-element.12.up_v, f32[512,3072]{1,0:T(8,128)S(1)} %get-tuple-element.13.master_v, ...), custom_call_target="tpu_custom_call" | custom-call | tf_op jit(solution)/shard_map/pallas_call | solution.py:407
